TPU v7x, 256 devices: a whole 4x4x8 slice. The times are simulated.
256 devices in a mesh: tile: 32 (over x, z), lev: 8 (over y, core).
Axes of the slice: x: 4, y: 4, z: 8, core: 2. Of those that a mesh axis runs over, the one named last changes fastest.
Arguments:
- krylov: bfloat16 [4, 16, 5, 8192, 128], P(None, 'lev', None, 'tile'), may hold values from -7 to 7, as said below
- adjoint: float32 [16, 5, 8192, 128], P('lev', None, 'tile'), may hold values from -200 to 200
- projected: float32 [4, 4], replicated, may hold values from -3 to 3
- stencil: bfloat16 [5, 16, 8192, 128], P(None, 'lev', 'tile'), may hold values from 0.19921875 to 1
- column_weight: float32 [2, 16, 8192, 128], P(None, 'lev', 'tile'), may hold values from 0.05 to 0.3
- seam_turns: int32 [32, 4], P('tile'), may hold values from 0 to 3
Outputs:
- updated: float32 [16, 5, 8192, 128], P('lev', None, 'tile')
Inputs may be any that keep to these rules, and one draw needn't show every extreme that they name: `krylov`: krylov vectors of order one.
All inputs are finite; a program needn't handle non-finite values.
Results may differ from a plain program's by a relative error of at most 0.0003.
Values sent between devices are 32-bit elements; how exact they have to be, the bound alone decides.
A program may use at most 128 MiB of HBM per device.

v0:
```python
import jax
import jax.numpy as jnp
from jax import lax
from jax.sharding import PartitionSpec as P

STRIDE = 4


def entering(x, axis, combine, identity):
    peers, here = (lax.axis_size(axis), lax.axis_index(axis))
    everything = lax.all_gather(x, axis)
    start = jnp.broadcast_to(jnp.asarray(identity, x.dtype), x.shape)

    def step(k, before):
        at = peers - 1 - k
        reached = at > here
        new = combine(before, everything[at])
        return jnp.where(reached, new, before)

    return lax.fori_loop(0, peers, step, start)


def with_halo(block, sides, width):
    for axis, dim in sides:
        count = lax.axis_size(axis)
        forward = [(i, i + 1) for i in range(count - 1)]
        forward.append((count - 1, 0))
        backward = [(target, source) for source, target in forward]
        low = lax.ppermute(
            lax.slice_in_dim(block, block.shape[dim] - width, None, axis=dim), axis, forward
        )
        high = lax.ppermute(lax.slice_in_dim(block, 0, width, axis=dim), axis, backward)
        block = jnp.concatenate([low, block, high], axis=dim)
    return block


def shifted(value, axis, steps):
    count = lax.axis_size(axis)
    pairs = [(source, (source + steps) % count) for source in range(count)]
    return lax.ppermute(value, axis, pairs)


def rotate(edge_strip, turning):
    flipped = jnp.where(turning % 2 == 1, edge_strip[..., ::-1], edge_strip)
    cosine = jnp.where(turning == 0, 1.0, jnp.where(turning == 2, -1.0, 0.0)).astype(
        edge_strip.dtype
    )
    sine_part = jnp.where(turning == 1, 1.0, jnp.where(turning == 3, -1.0, 0.0)).astype(
        edge_strip.dtype
    )
    wind_east = flipped[..., 2:3, :]
    wind_north = flipped[..., 3:4, :]
    turned_u = cosine * wind_east - sine_part * wind_north
    turned_v = sine_part * wind_east + cosine * wind_north
    return jnp.concatenate([flipped[..., :2, :], turned_u, turned_v, flipped[..., 4:, :]], axis=-2)


def add_pair(earlier, later):
    return earlier + later


def column_totals_below(totals):
    return entering(totals, "lev", add_pair, jnp.zeros_like(totals))


def apply_operator(field, stencil, column_weight, seam_turns):
    coeffs = stencil.astype(jnp.float32)[:, None, :, None]
    image = coeffs[0] * field
    plus_rows = coeffs[1] * field
    minus_rows = coeffs[2] * field
    edge_pairs = jnp.stack([minus_rows[..., 0, :], plus_rows[..., -1, :]], axis=0)
    padded = with_halo(edge_pairs, (("tile", 0),), 1)
    from_lower = rotate(padded[0], seam_turns[0, 0])
    from_upper = rotate(padded[3], seam_turns[0, 1])
    image = image + jnp.concatenate([from_lower[..., None, :], plus_rows[..., :-1, :]], axis=-2)
    image = image + jnp.concatenate([minus_rows[..., 1:, :], from_upper[..., None, :]], axis=-2)
    plus_cols = coeffs[3] * field
    minus_cols = coeffs[4] * field
    up_strip = shifted(plus_cols[..., -1], "tile", STRIDE)
    down_strip = shifted(minus_cols[..., 0], "tile", -STRIDE)
    up_strip = rotate(up_strip, seam_turns[0, 2])
    down_strip = rotate(down_strip, seam_turns[0, 3])
    image = image + jnp.concatenate([up_strip[..., None], plus_cols[..., :-1]], axis=-1)
    image = image + jnp.concatenate([minus_cols[..., 1:], down_strip[..., None]], axis=-1)
    carried = jnp.stack([field[:, :, 0], field[:, :, 3]], axis=2)
    totals = jnp.sum(carried, axis=1)
    below = column_totals_below(totals)
    suffix = jnp.cumsum(carried[:, ::-1], axis=1)[:, ::-1] + below[:, None]
    weights = jnp.moveaxis(column_weight, 0, 1)[None]
    scaled = suffix * weights
    zeros_part = jnp.zeros_like(scaled[:, :, 0])
    column_part = jnp.stack(
        [zeros_part, scaled[:, :, 0], zeros_part, zeros_part, scaled[:, :, 1]], axis=2
    )
    return image + column_part


def per_device(krylov, adjoint, projected, stencil, column_weight, seam_turns):
    vectors = krylov.astype(jnp.float32)
    partial_value = jnp.sum(vectors * adjoint[None], axis=(1, 2, 3, 4))
    count = (
        adjoint.shape[0]
        * adjoint.shape[1]
        * adjoint.shape[2]
        * adjoint.shape[3]
        * lax.axis_size("tile")
        * lax.axis_size("lev")
    )
    coupling = lax.psum(partial_value, ("tile", "lev")) / count
    mixing = jnp.sum(projected * coupling[:, None], axis=0)
    images = apply_operator(vectors, stencil, column_weight, seam_turns)
    total_image = jnp.sum(mixing[:, None, None, None, None] * images, axis=0)
    return adjoint + 0.5 * total_image


def solution(mesh):
    placed = (
        P(None, "lev", None, "tile", None),
        P("lev", None, "tile", None),
        P(),
        P(None, "lev", "tile", None),
        P(None, "lev", "tile", None),
        P("tile", None),
    )
    return jax.shard_map(
        per_device,
        mesh=mesh,
        in_specs=placed,
        out_specs=P("lev", None, "tile", None),
        check_vma=False,
    )
```

profile of v0, /device:TPU:1, one launch (start us, length us, event | category | flops | bytes accessed | tf_op | source)
XLA Modules:
  0.0 209.0 jit_solution(5820138084469214905)
XLA Ops:
  6.5 0.0 copy-start
  6.5 0.0 all-gather.3.cloned.1.call-start
  6.5 1.5 fusion.9
  8.0 0.0 copy-start.1
  8.0 2.6 %fusion.8 = (f32[4,2,256,128]{3,2,1,0:T(8,128)}, f32[4,2,2,256,128]{4,3,2,1,0:T(8,128)}) fusion(f32[4,2,1,256,128]{4,3,2,1,0:T(8,128)S(1)} %get-tuple-element.145, f32[4,2,1,256,128]{4,3,2,1,0:T(8,128)S(1)} %get-tuple-element.144), kind=kLoop, calls=%fused_computation.45 | loop fusion | flops 786432 | bytes 5242880 | tf_op jit(solution)/shard_map/reduce_sum | solution.py:86
  10.6 0.0 all-gather.3.cloned.1.call-update
  10.7 1.2 convert_element_type.7
  11.9 1.1 slice_bitcast_fusion.4
  12.9 0.0 copy-done.1
  12.9 10.5 %fusion = (f32[4]{0:T(128)S(1)}, f32[4,2,5,256,128]{4,3,2,1,0:T(8,128)}, f32[4,2,5,256,128]{4,3,2,1,0:T(8,128)}, f32[4,2,5,256,128]{4,3,2,1,0:T(8,128)}, f32[4,2,5,256,128]{4,3,2,1,0:T(8,128)}) fusion(bf16[4,2,5,256,128]{4,3,2,1,0:T(8,128)(2,1)S(1)} %copy-done.1, f32[2,5,256,128]{3,2,1,0:T(8,128)} %param.9, f32[2,256,128]{2,1,0:T(8,128)} %get-tuple-element.154, ...), kind=kLoop, calls=%fused_computation.7 | loop fusion | flops 9175036 | bytes 25952272 | tf_op jit(solution)/shard_map/reduce_sum | solution.py:100
  23.4 0.9 slice_bitcast_fusion.5
  24.3 8.7 %collective-permute-start.1 = (f32[1,4,2,5,128]{4,0,3,2,1:T(1,128)S(1)}, f32[1,4,2,5,128]{4,0,3,2,1:T(1,128)S(1)}, u32[]{:S(2)}, u32[]{:S(2)}) collective-permute-start(f32[1,4,2,5,128]{4,0,3,2,1:T(1,128)S(1)} %slice_bitcast_fusion.5), channel_id=1, source_target_pairs={{8,0},{16,8},{24,16},{32,24},{40,32},{48,40},{56,48},{64,56},{72,6... | collective-permute-start | bytes 61448 | tf_op jit(solution)/shard_map/ppermute | solution.py:32
  33.1 0.9 slice_bitcast_fusion.6
  34.0 0.1 collective-permute-start
  34.1 3.5 %copy.38 = f32[4,2,5,256,1]{3,1,2,0,4:T(2,128)S(1)} copy(f32[4,2,5,256,1]{4,3,2,1,0:T(8,128)} %bitcast.52) | data formatting | bytes 81920 | tf_op jit(solution)/shard_map/slice | solution.py:80
  37.6 2.8 %collective-permute-start.3 = (f32[4,2,5,256]{3,1,2,0:T(2,128)S(1)}, f32[4,2,5,256]{3,1,2,0:T(2,128)S(1)}, u32[]{:S(2)}, u32[]{:S(2)}) collective-permute-start(f32[4,2,5,256]{3,1,2,0:T(2,128)S(1)} %bitcast.63), channel_id=1, source_target_pairs={{0,224},{8,232},{16,240},{24,248},{32,0},{40,8},{48,16},{56,24},{6... | collective-permute-start | bytes 122888 | tf_op jit(solution)/shard_map/ppermute | solution.py:40
  40.4 6.3 %slice.169 = f32[4,2,5,256,1]{4,3,2,1,0:T(8,128)} slice(f32[4,2,5,256,128]{4,3,2,1,0:T(8,128)} %get-tuple-element.142), slice={[0:4], [0:2], [0:5], [0:256], [127:128]} | slice | bytes 81920 | tf_op jit(solution)/shard_map/slice | solution.py:79
  46.7 3.5 %copy.36 = f32[4,2,5,256,1]{3,1,2,0,4:T(2,128)S(1)} copy(f32[4,2,5,256,1]{4,3,2,1,0:T(8,128)} %slice.169) | data formatting | bytes 81920 | tf_op jit(solution)/shard_map/slice | solution.py:79
  50.2 2.7 %collective-permute-start.2 = (f32[4,2,5,256]{3,1,2,0:T(2,128)S(1)}, f32[4,2,5,256]{3,1,2,0:T(2,128)S(1)}, u32[]{:S(2)}, u32[]{:S(2)}) collective-permute-start(f32[4,2,5,256]{3,1,2,0:T(2,128)S(1)} %bitcast.62), channel_id=1, source_target_pairs={{0,32},{8,40},{16,48},{24,56},{32,64},{40,72},{48,80},{56,88},{64,... | collective-permute-start | bytes 122888 | tf_op jit(solution)/shard_map/ppermute | solution.py:40
  52.9 79.9 %psum.7 = f32[4]{0:T(128)S(1)} all-reduce(f32[4]{0:T(128)S(1)} %get-tuple-element.139), channel_id=1, replica_groups=mesh['tile'=32,'lev'=8] {'tile','lev'}, use_global_device_ids=true, to_apply=%region_1.0 | all-reduce | flops 4 | bytes 32 | tf_op jit(solution)/shard_map/psum | solution.py:109
  132.8 0.0 copy-done.3
  132.8 1.5 rev.22
  134.3 0.0 copy-done.6
  134.3 0.1 multiply_reduce_fusion
  134.4 3.2 %fusion.12 = f32[4,2,2,256,128]{4,3,2,1,0:T(8,128)} fusion(f32[4,2,2,256,128]{4,3,2,1,0:T(8,128)} %rev.22), kind=kOutput, calls=%fused_computation.49 | output fusion | flops 524288 | bytes 4194304 | tf_op jit(solution)/shard_map/jit(cumsum)/reduce_window_sum | solution.py:88
  137.6 0.0 copy-done.5
  137.6 0.7 fusion.11
  156.7 0.0 slice-start.1
  156.7 5.5 %slice.162 = f32[4,2,5,255,128]{4,3,2,1,0:T(8,128)} slice(f32[4,2,5,256,128]{4,3,2,1,0:T(8,128)} %get-tuple-element.141), slice={[0:4], [0:2], [0:5], [1:256], [0:128]} | slice | bytes 10444800 | tf_op jit(solution)/shard_map/slice | solution.py:76
  162.3 0.0 slice-done
  162.3 0.0 slice-done.1
  162.3 3.7 %slice.176 = f32[4,2,5,256,127]{4,3,2,1,0:T(8,128)} slice(f32[4,2,5,256,128]{4,3,2,1,0:T(8,128)S(1)} %bitcast.54), slice={[0:4], [0:2], [0:5], [0:256], [1:128]} | slice | bytes 10403840 | tf_op jit(solution)/shard_map/slice | solution.py:84
  166.0 0.1 pad.2.clone
  166.1 0.0 collective-permute-done.1
  166.2 0.1 rev.19
  166.3 0.0 collective-permute-done
  166.4 0.1 rev.18
  166.7 0.0 collective-permute-done.3
  166.7 0.3 rev.21
  167.1 3.1 %copy.39 = f32[4,2,5,256,1]{4,3,2,1,0:T(8,128)} copy(f32[4,2,5,256,1]{3,1,2,0,4:T(2,128)S(1)} %maximum_bitcast_fusion.1) | data formatting | bytes 81920 | tf_op jit(solution)/shard_map/broadcast_in_dim | solution.py:84
  170.2 0.0 collective-permute-done.2
  170.2 0.3 rev.20
  170.5 3.1 %copy.37 = f32[4,2,5,256,1]{4,3,2,1,0:T(8,128)} copy(f32[4,2,5,256,1]{3,1,2,0,4:T(2,128)S(1)} %maximum_bitcast_fusion) | data formatting | bytes 81920 | tf_op jit(solution)/shard_map/broadcast_in_dim | solution.py:83
  173.6 12.9 %while.16 = (s32[]{:T(128)}, f32[4,2,256,128]{3,2,1,0:T(8,128)S(1)}, s32[]{:T(128)}, f32[8,4,2,256,128]{4,3,2,1,0:T(8,128)}, s32[]{:T(128)}, /*index=5*/s32[]{:T(128)}, s32[]{:T(128)}, s32[]{:T(128)}) while((s32[]{:T(128)}, f32[4,2,256,128]{3,2,1,0:T(8,128)S(1)}, s32[]{:T(128)}, f32[8,4,2,256,128]{4,3,2,1,0:T(8,128)}, s32[]{:T(128)}, ...), condition=%wide.region_6.7_spmd.clone, body=%wide.region_5.6_spmd.clone.sunk | while | flops 786440 | bytes 3145891 | solution.py:20
  173.6 1.6 add_select_fusion.2
  175.2 1.6 add_select_fusion.2
  176.9 1.6 add_select_fusion.2
  178.5 1.6 add_select_fusion.2
  180.1 1.6 add_select_fusion.2
  181.7 1.6 add_select_fusion.2
  183.3 1.6 add_select_fusion.2
  185.0 1.6 add_select_fusion.2
  186.6 0.0 slice-start.2
  186.6 0.0 copy-start.2
  186.6 0.0 copy-done
  186.6 0.0 slice-start.3
  186.6 1.9 add_multiply_fusion
  188.5 0.2 fusion.10
  188.7 0.6 slice-done.2
  189.4 0.8 copy-done.2
  190.2 0.2 slice-done.3
  190.4 10.5 %fusion.7 = f32[2,5,256,128]{3,2,1,0:T(8,128)S(1)} fusion(bf16[4,2,5,256,128]{4,3,2,1,0:T(8,128)(2,1)S(1)} %copy-done.2, f32[4,2,5,255,128]{4,3,2,1,0:T(8,128)} %bitcast.58, f32[4,2,5,1,128]{4,3,2,1,0:T(1,128)S(1)} %copy.33, f32[4,2,5,1,128]{4,3,2,1,0:T(1,128)S(1)} %copy.35, f32[4,2,5,255,128]{4,3,2,1,0:T(8,128)} %slice.162, ...), kind=kLoop, calls=%fused_computation.14 | loop fusion | flops 20643840 | bytes 27263032 | tf_op jit(solution)/shard_map/reduce_sum | solution.py:112
  201.0 0.0 copy-done.4
  201.0 1.2 multiply_add_fusion
  (32 shorter events, 0.3 us)
Async XLA Ops:
  6.5 180.0 %copy-start = (f32[2,2,256,128]{3,2,1,0:T(8,128)S(1)}, f32[2,2,256,128]{3,2,1,0:T(8,128)}, u32[]{:S(2)}) copy-start(f32[2,2,256,128]{3,2,1,0:T(8,128)} %param.12) | copy-start | bytes 1572868
  6.5 167.1 %all-gather.3.cloned.1.call-start = ((), (), s32[]{:S(2)}) async-start(), calls=%async_computation | async-start | bytes 9437184 | tf_op jit(solution)/shard_map/all_gather | solution.py:11
  8.0 4.9 %copy-start.1 = (bf16[4,2,5,256,128]{4,3,2,1,0:T(8,128)(2,1)S(1)}, bf16[4,2,5,256,128]{4,3,2,1,0:T(8,128)(2,1)}, u32[]{:S(2)}) copy-start(bf16[4,2,5,256,128]{4,3,2,1,0:T(8,128)(2,1)} %param.8) | copy-start | bytes 7864324
  24.3 141.8 %collective-permute-start.1 = (f32[1,4,2,5,128]{4,0,3,2,1:T(1,128)S(1)}, f32[1,4,2,5,128]{4,0,3,2,1:T(1,128)S(1)}, u32[]{:S(2)}, u32[]{:S(2)}) collective-permute-start(f32[1,4,2,5,128]{4,0,3,2,1:T(1,128)S(1)} %slice_bitcast_fusion.5), channel_id=1, source_target_pairs={{8,0},{16,8},{24,16},{32,24},{40,32},{48,40},{56,48},{64,56},{72,6... | collective-permute-start | bytes 61448 | tf_op jit(solution)/shard_map/ppermute | solution.py:32
  34.0 132.3 %collective-permute-start = (f32[1,4,2,5,128]{4,0,3,2,1:T(1,128)S(1)}, f32[1,4,2,5,128]{4,0,3,2,1:T(1,128)S(1)}, u32[]{:S(2)}, u32[]{:S(2)}) collective-permute-start(f32[1,4,2,5,128]{4,0,3,2,1:T(1,128)S(1)} %slice_bitcast_fusion.6), channel_id=1, source_target_pairs={{0,8},{8,16},{16,24},{24,32},{32,40},{40,48},{48,56},{56,64},{64,7... | collective-permute-start | bytes 61448 | tf_op jit(solution)/shard_map/ppermute | solution.py:29
  37.6 129.1 %collective-permute-start.3 = (f32[4,2,5,256]{3,1,2,0:T(2,128)S(1)}, f32[4,2,5,256]{3,1,2,0:T(2,128)S(1)}, u32[]{:S(2)}, u32[]{:S(2)}) collective-permute-start(f32[4,2,5,256]{3,1,2,0:T(2,128)S(1)} %bitcast.63), channel_id=1, source_target_pairs={{0,224},{8,232},{16,240},{24,248},{32,0},{40,8},{48,16},{56,24},{6... | collective-permute-start | bytes 122888 | tf_op jit(solution)/shard_map/ppermute | solution.py:40
  46.7 86.1 %copy-start.3 = (f32[4,2,2,256,128]{4,3,2,1,0:T(8,128)S(1)}, f32[4,2,2,256,128]{4,3,2,1,0:T(8,128)}, u32[]{:S(2)}) copy-start(f32[4,2,2,256,128]{4,3,2,1,0:T(8,128)} %get-tuple-element.149) | copy-start | bytes 6291460
  46.7 87.6 %copy-start.6 = (f32[4,4]{1,0:T(4,128)S(1)}, f32[4,4]{1,0:T(4,128)}, u32[]{:S(2)}) copy-start(f32[4,4]{1,0:T(4,128)} %param.10) | copy-start | bytes 196
  50.2 87.4 %copy-start.5 = (s32[1,4]{1,0:T(1,128)S(1)}, s32[1,4]{1,0:T(1,128)}, u32[]{:S(2)}) copy-start(s32[1,4]{1,0:T(1,128)} %param.13) | copy-start | bytes 52
  50.2 120.0 %collective-permute-start.2 = (f32[4,2,5,256]{3,1,2,0:T(2,128)S(1)}, f32[4,2,5,256]{3,1,2,0:T(2,128)S(1)}, u32[]{:S(2)}, u32[]{:S(2)}) collective-permute-start(f32[4,2,5,256]{3,1,2,0:T(2,128)S(1)} %bitcast.62), channel_id=1, source_target_pairs={{0,32},{8,40},{16,48},{24,56},{32,64},{40,72},{48,80},{56,88},{64,... | collective-permute-start | bytes 122888 | tf_op jit(solution)/shard_map/ppermute | solution.py:40
  134.4 27.9 %slice-start = ((s8[5242880]{0:T(1024)(128)(4,1)}), s8[1048576]{0:T(1024)(128)(4,1)S(1)}, s32[]{:S(2)}) async-start(s8[5242880]{0:T(1024)(128)(4,1)} %bitcast.53), calls=%async_computation.1 | async-start | bytes 2097152
  156.7 5.5 %slice-start.1 = ((s8[5242880]{0:T(1024)(128)(4,1)}), s8[4194304]{0:T(1024)(128)(4,1)S(1)}, s32[]{:S(2)}) async-start(s8[5242880]{0:T(1024)(128)(4,1)} %bitcast.53), calls=%async_computation.2 | async-start | bytes 8388608
  186.6 2.8 %slice-start.2 = ((s8[5242880]{0:T(1024)(128)(4,1)}), s8[4194304]{0:T(1024)(128)(4,1)S(1)}, s32[]{:S(2)}) async-start(s8[5242880]{0:T(1024)(128)(4,1)} %bitcast.55), calls=%async_computation.3 | async-start | bytes 8388608
  186.6 3.6 %copy-start.2 = (bf16[4,2,5,256,128]{4,3,2,1,0:T(8,128)(2,1)S(1)}, bf16[4,2,5,256,128]{4,3,2,1,0:T(8,128)(2,1)}, u32[]{:S(2)}) copy-start(bf16[4,2,5,256,128]{4,3,2,1,0:T(8,128)(2,1)} %param.8) | copy-start | bytes 7864324
  186.6 3.8 %slice-start.3 = ((s8[5242880]{0:T(1024)(128)(4,1)}), s8[1048576]{0:T(1024)(128)(4,1)S(1)}, s32[]{:S(2)}) async-start(s8[5242880]{0:T(1024)(128)(4,1)} %bitcast.55), calls=%async_computation.4 | async-start | bytes 2097152
  190.4 10.5 %copy-start.4 = (f32[2,5,256,128]{3,2,1,0:T(8,128)S(1)}, f32[2,5,256,128]{3,2,1,0:T(8,128)}, u32[]{:S(2)}) copy-start(f32[2,5,256,128]{3,2,1,0:T(8,128)} %param.9) | copy-start | bytes 3932164
Sparse Core Ops, SparseCore 0:
  10.8 56.5 all-gather.2
where the time goes:
time: 210 us; the launch traced here: 209 us
  blocking collectives  79.9 us (38%)
  other arithmetic  44.1 us (21%)
  local copies, waits for them, and re-layouts  38.1 us (18%)
  between operations  32.3 us (15%)
  starting transfers between devices  14.4 us (7%)
    psum x1, blocking collectives, per_device(): coupling = lax.psum(partial_value, ('tile', 'lev')) / count  79.9 us
    select_n x8, other arithmetic, step(): return jnp.where(reached, new, before)  12.7 us
    reduce_sum x1, other arithmetic, per_device(): total_image = jnp.sum(mixing[:, None, None, None, None] * images, axis=0)  10.5 us
    reduce_sum x1, other arithmetic, per_device(): partial_value = jnp.sum(vectors * adjoint[None], axis=(1, 2, 3, 4))  10.5 us
    slice x2, local copies, waits for them, and re-layouts, apply_operator(): up_strip = shifted(plus_cols[..., -1], 'tile', STRIDE)  9.79 us
    ppermute x1, starting transfers between devices, with_halo(): lax.ppermute(lax.slice_in_dim(block, 0, width, axis=dim), axis, backward)  8.73 us
    ppermute x2, starting transfers between devices, shifted(): return lax.ppermute(value, axis, pairs)  5.54 us
    slice x1, local copies, waits for them, and re-layouts, apply_operator(): minus_rows[..., 1:, :]  5.53 us
  transfers between devices with their start and end apart: 5, of which 0 were waited for; matrix products, arithmetic and copies ran while one was open for 24% of the time, Pallas kernels for 0%

commit v1 on v0

v1 whole, which is shorter than its diff:
```python
import functools

import jax
import jax.numpy as jnp
from jax import lax
from jax.experimental import pallas as pl
from jax.experimental.pallas import tpu as pltpu
from jax.sharding import PartitionSpec as P

MESH = pl.DeviceIdType.MESH
STRIDE = 4
KRYLOV = 4
FIELDS = 5
LEVELS = 2
ROWS = 256
COLS = 128
HALF = ROWS // 2
CHUNKS = 4
PART = 2 * HALF // CHUNKS
NX, NZ, NY, NC = 4, 8, 4, 2
PAIRS = LEVELS * FIELDS
COUNT = 16 * FIELDS * 8192 * COLS


def ring(d, n):
    return min(d % n, (-d) % n)


GROUP_XY = sorted(
    [(dx, dy) for dx in range(NX) for dy in range(NY) if (dx, dy) != (0, 0)],
    key=lambda o: -(ring(o[0], NX) + ring(o[1], NY)),
)
GROUP_ZC = sorted(
    [(dz, dc) for dz in range(NZ) for dc in range(NC) if (dz, dc) != (0, 0)],
    key=lambda o: -(ring(o[0], NZ) + 0.5 * o[1]),
)


def splat_sum(x):
    return jnp.sum(jnp.sum(x, axis=0, keepdims=True), axis=1, keepdims=True)


def turned(strip, turn, lane_flip):
    odd = lax.rem(turn, 2) == 1
    cosine = jnp.where(turn == 0, 1.0, jnp.where(turn == 2, -1.0, 0.0)).astype(jnp.float32)
    sine = jnp.where(turn == 1, 1.0, jnp.where(turn == 3, -1.0, 0.0)).astype(jnp.float32)
    halves = [strip[:, i : i + COLS] for i in range(0, strip.shape[1], COLS)]
    back = [jnp.take_along_axis(h, lane_flip, axis=1) for h in halves[::-1]]
    pair = lax.broadcasted_iota(jnp.int32, halves[0].shape, 0)
    field = lax.rem(pair, FIELDS)
    out = []
    for h, b in zip(halves, back):
        x = jnp.where(odd, b, h)
        after = pltpu.roll(x, x.shape[0] - 1, 0)
        before = pltpu.roll(x, 1, 0)
        out.append(
            jnp.where(
                field == 2,
                cosine * x - sine * after,
                jnp.where(field == 3, sine * before + cosine * x, x),
            )
        )
    return out


def kernel(
    k_hbm, a_hbm, s_hbm, w_hbm, proj, seam,
    out,
    kv, av, sv, wv, comb,
    ls_own, ls_send, ls_recv,
    total, mine, other, relay, buf_a, buf_b, below_send, below,
    row1, row2, got1, got2,
    row_send, row_got, col_mix, col_t, col_send, col_got, col_back, col_add,
    load_sem, red_send, red_recv, ls_sem, y_send, a_sem, b_sem, below_sem, edge_sem,
):
    t, l = lax.axis_index("tile"), lax.axis_index("lev")
    x, z, y, c = t // NZ, lax.rem(t, NZ), l // NC, lax.rem(l, NC)
    f32 = jnp.float32

    loads = []
    for f in range(FIELDS):
        loads.append(pltpu.make_async_copy(k_hbm.at[:, :, f], kv.at[:, :, f], load_sem.at[f]))
        loads.append(pltpu.make_async_copy(a_hbm.at[:, f], av.at[:, f], load_sem.at[FIELDS + f]))
    load_s = pltpu.make_async_copy(s_hbm, sv, load_sem.at[2 * FIELDS])
    load_w = pltpu.make_async_copy(w_hbm, wv, load_sem.at[2 * FIELDS + 1])
    order = [0, 3, 1, 2, 4]
    for f in order:
        loads[2 * f].start()
        loads[2 * f + 1].start()

    def at_xy(dx, dy):
        return (lax.rem(x + dx, NX) * NZ + z, lax.rem(y + dy, NY) * NC + c)

    def at_zc(dz, dc):
        return (x * NZ + lax.rem(z + dz, NZ), y * NC + lax.rem(c + dc, NC))

    def at_tile(d):
        return (lax.rem(t + d + NX * NZ, NX * NZ), l)

    peers = [at_xy(*o) for o in GROUP_XY] + [at_zc(*o) for o in GROUP_ZC]
    peers += [at_tile(d) for d in (STRIDE, -STRIDE, 1, -1)]
    barrier = pltpu.get_barrier_semaphore()
    for peer in peers:
        pl.semaphore_signal(barrier, inc=1, device_id=peer, device_id_type=MESH)
    load_s.start()
    load_w.start()

    zero8 = jnp.zeros((8, COLS), f32)
    sums = (zero8,) * KRYLOV
    keep, give = c * HALF, (1 - c) * HALF
    for f in order:
        loads[2 * f].wait()
        loads[2 * f + 1].wait()

        def dots(i, sums, f=f):
            lev, blk = i // 16, lax.rem(i, 16)
            at = pl.ds(pl.multiple_of(blk * 16, 16), 16)
            a = av[lev, f, at, :]
            out_sums = []
            for k in range(KRYLOV):
                prod = kv[k, lev, f, at, :].astype(f32) * a
                out_sums.append(sums[k] + prod[0:8] + prod[8:16])
            return tuple(out_sums)

        sums = lax.fori_loop(0, LEVELS * 16, dots, sums, unroll=4)
        if f in (0, 3):
            g = f // 3

            def level_sums(k, _, f=f, g=g):
                for dst, start in ((ls_send, give), (ls_own, keep)):
                    at = pl.ds(pl.multiple_of(start, HALF), HALF)
                    dst[k, g] = kv[k, 0, f, at, :].astype(f32) + kv[k, 1, f, at, :].astype(f32)
                return 0

            lax.fori_loop(0, KRYLOV, level_sums, 0)

    lane1 = lax.broadcasted_iota(jnp.int32, (1, COLS), 1)
    mine_row = jnp.zeros((1, COLS), f32)
    for k in range(KRYLOV):
        mine_row = jnp.where(lane1 == k, splat_sum(sums[k]), mine_row)
    row1[...] = mine_row

    pl.semaphore_wait(barrier, len(peers))

    for j, o in enumerate(GROUP_XY):
        pltpu.make_async_remote_copy(
            src_ref=row1, dst_ref=got1.at[j], send_sem=red_send.at[0], recv_sem=red_recv.at[0],
            device_id=at_xy(*o), device_id_type=MESH,
        ).start()
    swap = pltpu.make_async_remote_copy(
        src_ref=ls_send, dst_ref=ls_recv, send_sem=ls_sem.at[0], recv_sem=ls_sem.at[1],
        device_id=at_zc(0, 1), device_id_type=MESH,
    )
    swap.start()
    pltpu.make_async_copy(got1, got1, red_recv.at[0]).wait()
    stage = row1[...]
    for j in range(len(GROUP_XY)):
        stage = stage + got1[j]
    row2[...] = stage
    for j, o in enumerate(GROUP_ZC):
        pltpu.make_async_remote_copy(
            src_ref=row2, dst_ref=got2.at[j], send_sem=red_send.at[1], recv_sem=red_recv.at[1],
            device_id=at_zc(*o), device_id_type=MESH,
        ).start()
    load_s.wait()
    load_w.wait()
    swap.wait()
    pltpu.make_async_copy(got1, got1, red_send.at[0]).wait()
    pltpu.make_async_copy(got2, got2, red_recv.at[1]).wait()
    stage = row2[...]
    for j in range(len(GROUP_ZC)):
        stage = stage + got2[j]
    coupling = [
        jnp.sum(jnp.where(lane1 == k, stage, 0.0), axis=1, keepdims=True) * (0.5 / COUNT)
        for k in range(KRYLOV)
    ]
    mix = []
    for j in range(KRYLOV):
        m = proj[0, j] * coupling[0]
        for k in range(1, KRYLOV):
            m = m + proj[k, j] * coupling[k]
        mix.append(jnp.broadcast_to(m, (8, COLS)))

    def mixed(parts):
        acc = None
        for m, p in zip(mix, parts):
            rows = p.shape[0]
            term = jnp.concatenate([m] * (rows // 8), axis=0) * p
            acc = term if acc is None else acc + term
        return acc

    for j in range(CHUNKS):
        g, at = (j * PART) // HALF, pl.ds((j * PART) % HALF, PART)
        m = mixed([ls_own[k, g, at, :] for k in range(KRYLOV)])
        o = mixed([ls_recv[k, g, at, :] for k in range(KRYLOV)])
        mine[j] = m
        other[j] = o
        total[j] = m + o

        def down(src, dst, slot, sem):
            return pltpu.make_async_remote_copy(
                src_ref=src, dst_ref=dst, send_sem=y_send.at[slot], recv_sem=sem,
                device_id=at_xy(0, NY - 1), device_id_type=MESH,
            )

        def up(src, dst, slot, sem):
            return pltpu.make_async_remote_copy(
                src_ref=src, dst_ref=dst, send_sem=y_send.at[slot], recv_sem=sem,
                device_id=at_xy(0, 1), device_id_type=MESH,
            )

        @pl.when(y >= 2)
        def _(j=j):
            down(total.at[j], buf_a.at[j], j, a_sem.at[j]).start()

        @pl.when(y == NY - 1)
        def _(j=j):
            up(total.at[j], buf_b.at[j], CHUNKS + j, b_sem.at[j]).start()

    def combine(i, _):
        for f in range(FIELDS):
            lev, blk = i // 8, lax.rem(i, 8)
            at = pl.ds(pl.multiple_of(blk * 32, 32), 32)
            comb[lev * FIELDS + f, at, :] = mixed(
                [kv[k, lev, f, at, :].astype(f32) for k in range(KRYLOV)]
            )
        return 0

    lax.fori_loop(0, LEVELS * 8, combine, 0)

    lane = lax.broadcasted_iota(jnp.int32, (ROWS, COLS), 1)
    for p in range(PAIRS):
        lev = p // FIELDS
        row_send[0, p : p + 1, :] = (
            sv[1, lev, ROWS - 16 : ROWS, :].astype(f32)[15:16] * comb[p, ROWS - 1 : ROWS, :]
        )
        row_send[1, p : p + 1, :] = sv[2, lev, 0:16, :].astype(f32)[0:1] * comb[p, 0:1, :]

    def strips(p, _):
        lev = p // FIELDS
        field = comb[p]
        both = jnp.where(
            lane == 0, sv[4, lev].astype(f32) * field, sv[3, lev].astype(f32) * field
        )
        moved = pltpu.roll(both, 2 * p + 1, 1)
        col_mix[...] = jnp.where(lane // 2 == p, moved, col_mix[...])
        return 0

    col_mix[...] = jnp.zeros((ROWS, COLS), f32)
    row_send[:, PAIRS:, :] = jnp.zeros((2, 16 - PAIRS, COLS), f32)
    lax.fori_loop(0, PAIRS, strips, 0)
    for i in range(2):
        col_t[...] = jnp.transpose(col_mix[i * COLS : (i + 1) * COLS, :])
        for s in range(2):
            col_send[s, :, i * COLS : (i + 1) * COLS] = col_t[pl.ds(s, 16, stride=2), :]

    edges = []
    for s, (src, dst, d) in enumerate(
        (
            (row_send.at[0], row_got.at[0], 1),
            (row_send.at[1], row_got.at[1], -1),
            (col_send.at[0], col_got.at[0], STRIDE),
            (col_send.at[1], col_got.at[1], -STRIDE),
        )
    ):
        edges.append(
            pltpu.make_async_remote_copy(
                src_ref=src, dst_ref=dst, send_sem=edge_sem.at[s], recv_sem=edge_sem.at[4 + s],
                device_id=at_tile(d), device_id_type=MESH,
            )
        )
    for s in (2, 3, 0, 1):
        edges[s].start()

    for j in range(CHUNKS):

        @pl.when(y == 1)
        def _(j=j):
            down(total.at[j], buf_a.at[j], j, a_sem.at[j]).wait_recv()
            relay[j] = total[j] + buf_a[j]
            down(relay.at[j], buf_a.at[j], j, a_sem.at[j]).start()

        @pl.when(y == 0)
        def _(j=j):
            up(total.at[j], buf_b.at[j], CHUNKS + j, b_sem.at[j]).wait_recv()
            up(buf_b.at[j], buf_b.at[j], CHUNKS + j, b_sem.at[j]).start()

    row = lax.broadcasted_iota(jnp.int32, (ROWS, COLS), 0)

    def interior(p, _):
        lev, f = p // FIELDS, lax.rem(p, FIELDS)
        field = comb[p]
        acc = av[lev, f] + sv[0, lev].astype(f32) * field
        acc = acc + jnp.where(row == 0, 0.0, pltpu.roll(sv[1, lev].astype(f32) * field, 1, 0))
        acc = acc + jnp.where(
            row == ROWS - 1, 0.0, pltpu.roll(sv[2, lev].astype(f32) * field, ROWS - 1, 0)
        )
        acc = acc + jnp.where(lane == 0, 0.0, pltpu.roll(sv[3, lev].astype(f32) * field, 1, 1))
        acc = acc + jnp.where(
            lane == COLS - 1, 0.0, pltpu.roll(sv[4, lev].astype(f32) * field, COLS - 1, 1)
        )
        out[lev, f] = acc
        return 0

    lax.fori_loop(0, PAIRS, interior, 0)

    for j in range(CHUNKS):

        @pl.when(y == NY - 1)
        def _(j=j):
            relay[j] = jnp.zeros((PART, COLS), f32)

        @pl.when(y == 2)
        def _(j=j):
            down(total.at[j], buf_a.at[j], j, a_sem.at[j]).wait_recv()
            relay[j] = buf_a[j]

        @pl.when(y == 1)
        def _(j=j):
            up(total.at[j], buf_b.at[j], CHUNKS + j, b_sem.at[j]).wait_recv()
            buf_b[j] = buf_a[j] + buf_b[j]

        @pl.when(y == 0)
        def _(j=j):
            down(total.at[j], buf_a.at[j], j, a_sem.at[j]).wait_recv()
            relay[j] = buf_a[j] + buf_b[j]

        higher = jnp.where(y == 1, buf_b[j], relay[j])
        below_send[j] = jnp.where(c == 1, higher + mine[j], higher)
        pltpu.make_async_remote_copy(
            src_ref=below_send.at[j], dst_ref=below.at[1, j], send_sem=below_sem.at[j],
            recv_sem=below_sem.at[CHUNKS + j], device_id=at_zc(0, 1), device_id_type=MESH,
        ).start()
        below[0, j] = jnp.where(c == 1, higher, higher + other[j])

    lane_flip = COLS - 1 - lax.broadcasted_iota(jnp.int32, (16, COLS), 1)
    for s in range(4):
        edges[s].wait()
    for s in range(2):
        strip = turned(row_got[s], seam[0, s], lane_flip)[0]
        row_got[s] = strip
        parts = turned(col_got[s], seam[0, 2 + s], lane_flip)
        for i in range(2):
            col_back[i, pl.ds(1 - s, 16, stride=2), :] = parts[i]
    col_add[0:COLS, :] = jnp.transpose(col_back[0])
    col_add[COLS:ROWS, :] = jnp.transpose(col_back[1])

    def edge_add(p, _):
        lev, f = p // FIELDS, lax.rem(p, FIELDS)
        moved = pltpu.roll(col_add[...], COLS - 1 - 2 * p, 1)
        ends = (lane == 0) | (lane == COLS - 1)
        out[lev, f] = out[lev, f] + jnp.where(ends, moved, 0.0)
        return 0

    lax.fori_loop(0, PAIRS, edge_add, 0)
    for p in range(PAIRS):
        lev, f = p // FIELDS, p % FIELDS
        out[lev, f, 0:1, :] = out[lev, f, 0:1, :] + row_got[0, p : p + 1, :]
        out[lev, f, ROWS - 1 : ROWS, :] = out[lev, f, ROWS - 1 : ROWS, :] + row_got[1, p : p + 1, :]

    for side in range(2):
        start = keep if side == 0 else give
        for j in range(CHUNKS):
            if side == 1:
                pltpu.make_async_remote_copy(
                    src_ref=below_send.at[j], dst_ref=below.at[1, j], send_sem=below_sem.at[j],
                    recv_sem=below_sem.at[CHUNKS + j], device_id=at_zc(0, 1), device_id_type=MESH,
                ).wait()
            g = (j * PART) // HALF
            at = pl.ds(pl.multiple_of(start + (j * PART) % HALF, PART), PART)
            upper = below[side, j] + comb[FIELDS + 3 * g, at, :]
            lower = upper + comb[3 * g, at, :]
            f = 1 + 3 * g
            out[1, f, at, :] = out[1, f, at, :] + wv[g, 1, at, :] * upper
            out[0, f, at, :] = out[0, f, at, :] + wv[g, 0, at, :] * lower

    pltpu.make_async_copy(got2, got2, red_send.at[1]).wait()
    for j in range(CHUNKS):

        @pl.when(y >= 1)
        def _(j=j):
            down(total.at[j], buf_a.at[j], j, a_sem.at[j]).wait_send()

        @pl.when((y == NY - 1) | (y == 0))
        def _(j=j):
            up(total.at[j], buf_b.at[j], CHUNKS + j, b_sem.at[j]).wait_send()


def per_device(krylov, adjoint, projected, stencil, column_weight, seam_turns):
    f32 = jnp.float32
    vm = pltpu.VMEM
    dma = pltpu.SemaphoreType.DMA
    anywhere = pl.BlockSpec(memory_space=pltpu.HBM)
    scalars = pl.BlockSpec(memory_space=pltpu.SMEM)
    return pl.pallas_call(
        kernel,
        out_shape=jax.ShapeDtypeStruct(adjoint.shape, f32),
        in_specs=[anywhere] * 4 + [scalars] * 2,
        out_specs=pl.BlockSpec(memory_space=pltpu.VMEM),
        scratch_shapes=[
            vm(krylov.shape, krylov.dtype), vm(adjoint.shape, f32), vm(stencil.shape, stencil.dtype),
            vm(column_weight.shape, f32), vm((PAIRS, ROWS, COLS), f32),
            vm((KRYLOV, 2, HALF, COLS), f32), vm((KRYLOV, 2, HALF, COLS), f32),
            vm((KRYLOV, 2, HALF, COLS), f32),
            vm((CHUNKS, PART, COLS), f32), vm((CHUNKS, PART, COLS), f32), vm((CHUNKS, PART, COLS), f32),
            vm((CHUNKS, PART, COLS), f32), vm((CHUNKS, PART, COLS), f32), vm((CHUNKS, PART, COLS), f32),
            vm((CHUNKS, PART, COLS), f32), vm((2, CHUNKS, PART, COLS), f32),
            vm((1, COLS), f32), vm((1, COLS), f32),
            vm((len(GROUP_XY), 1, COLS), f32), vm((len(GROUP_ZC), 1, COLS), f32),
            vm((2, 16, COLS), f32), vm((2, 16, COLS), f32), vm((ROWS, COLS), f32), vm((COLS, COLS), f32),
            vm((2, 16, ROWS), f32), vm((2, 16, ROWS), f32), vm((2, COLS, COLS), f32), vm((ROWS, COLS), f32),
            dma((2 * FIELDS + 2,)), dma((2,)), dma((2,)), dma((2,)), dma((2 * CHUNKS,)), dma((CHUNKS,)),
            dma((CHUNKS,)), dma((2 * CHUNKS,)), dma((8,)),
        ],
        name="step",
        compiler_params=pltpu.CompilerParams(
            collective_id=0, has_side_effects=True, vmem_limit_bytes=60 << 20
        ),
    )(krylov, adjoint, stencil, column_weight, projected, seam_turns)


def solution(mesh):
    placed = (
        P(None, "lev", None, "tile", None),
        P("lev", None, "tile", None),
        P(),
        P(None, "lev", "tile", None),
        P(None, "lev", "tile", None),
        P("tile", None),
    )
    return jax.shard_map(
        per_device,
        mesh=mesh,
        in_specs=placed,
        out_specs=P("lev", None, "tile", None),
        check_vma=False,
    )
```

time: 210 us -> 34.2 us (0.16)
  blocking collectives: 79.9 us -> 0 us
  other arithmetic: 44.1 us -> 0 us
  local copies, waits for them, and re-layouts: 38.1 us -> 2.47 us
  between operations: 32.3 us -> 0.01 us
  Pallas kernels: 0 us -> 31.6 us
  starting transfers between devices: 14.4 us -> 0 us
    psum x1 -> x0, blocking collectives: 79.9 us -> none  [per_device(): coupling = lax.psum(partial_value, ('tile', 'lev')) / count]
    pallas_call x0 -> x1, Pallas kernels: none -> 31.6 us  [per_device(): pl.pallas_call(kernel, out_shape=jax.ShapeDtypeStruct(adjoint.shape, f32)...]
    slice x12 -> x0, local copies, waits for them, and re-layouts: 24.8 us -> none  [the longest x2 9.79 us: apply_operator(): up_strip = shifted(plus_cols[..., -1], 'tile', STRIDE)]
    reduce_sum x4 -> x0, other arithmetic: 23.7 us -> none  [the longest x1 10.5 us: per_device(): total_image = jnp.sum(mixing[:, None, None, None, None] * images, axis=0)]
    ppermute x4 -> x0, starting transfers between devices: 14.4 us -> none  [the longest x1 8.73 us: with_halo(): lax.ppermute(lax.slice_in_dim(block, 0, width, axis=dim), axis, backward)]
    select_n x12 -> x0, other arithmetic: 12.8 us -> none  [the longest x8 12.7 us: step(): return jnp.where(reached, new, before)]
    broadcast_in_dim x4 -> x0, local copies, waits for them, and re-layouts: 6.23 us -> none  [the longest x1 3.1 us: apply_operator(): down_strip[..., None]]
    another operation x1 -> x0, other arithmetic: 3.19 us -> none  [apply_operator(): suffix = jnp.cumsum(carried[:, ::-1], axis=1)[:, ::-1] + below[:, None]]
  transfers between devices with their start and end apart: 5 -> 0, of which waited for: 0 -> 0; matrix products, arithmetic and copies ran while one was open for 24% -> 0% of each run, Pallas kernels for 0% -> 0%
where the time goes in v1:
time: 34.2 us; the launch traced here: 34.1 us
  Pallas kernels  31.6 us (92%)
  local copies, waits for them, and re-layouts  2.47 us (7%)
    pallas_call x1, Pallas kernels, per_device(): pl.pallas_call(kernel, out_shape=jax.ShapeDtypeStruct(adjoint.shape, f32)...  31.6 us
    unnamed x1, local copies, waits for them, and re-layouts  2.47 us

profile of v1, /device:TPU:1, one launch (start us, length us, event | category | flops | bytes accessed | tf_op | source)
XLA Modules:
  0.0 34.1 jit_solution(15919303444197880362)
XLA Ops:
  0.0 31.6 %step.1 = f32[2,5,256,128]{3,2,1,0:T(8,128)} custom-call(bf16[4,2,5,256,128]{4,3,2,1,0:T(8,128)(2,1)} %k_hbm.1, f32[2,5,256,128]{3,2,1,0:T(8,128)} %a_hbm.1, bf16[5,2,256,128]{3,2,1,0:T(8,128)(2,1)} %s_hbm.1, f32[2,2,256,128]{3,2,1,0:T(8,128)} %w_hbm.1, f32[4,4]{1,0:T(4,128)} %proj.1, s32[1,4]{1,0:T(1,128)} %seam.1), custom_call_target="tpu_custom_call" | custom-call | tf_op jit(solution)/shard_map/step/pallas_call | solution.py:395
  31.6 2.5 %copy.8 = f32[2,5,256,128]{3,2,1,0:T(8,128)} copy(f32[2,5,256,128]{3,2,1,0:T(8,128)} %step.1) | data formatting | bytes 2621440

commit v2 on v1

--- a/solution.py
+++ b/solution.py
@@ -64,9 +64,9 @@
 
 
 def kernel(
-    k_hbm, a_hbm, s_hbm, w_hbm, proj, seam,
+    k_hbm, a_hbm, s_hbm, w_hbm, p_hbm, t_hbm,
     out,
-    kv, av, sv, wv, comb,
+    kv, av, sv, wv, proj, seam, comb,
     ls_own, ls_send, ls_recv,
     total, mine, other, relay, buf_a, buf_b, below_send, below,
     row1, row2, got1, got2,
@@ -83,6 +83,8 @@
         loads.append(pltpu.make_async_copy(a_hbm.at[:, f], av.at[:, f], load_sem.at[FIELDS + f]))
     load_s = pltpu.make_async_copy(s_hbm, sv, load_sem.at[2 * FIELDS])
     load_w = pltpu.make_async_copy(w_hbm, wv, load_sem.at[2 * FIELDS + 1])
+    load_p = pltpu.make_async_copy(p_hbm, proj, load_sem.at[2 * FIELDS + 2])
+    load_t = pltpu.make_async_copy(t_hbm, seam, load_sem.at[2 * FIELDS + 3])
     order = [0, 3, 1, 2, 4]
     for f in order:
         loads[2 * f].start()
@@ -104,6 +106,8 @@
         pl.semaphore_signal(barrier, inc=1, device_id=peer, device_id_type=MESH)
     load_s.start()
     load_w.start()
+    load_p.start()
+    load_t.start()
 
     zero8 = jnp.zeros((8, COLS), f32)
     sums = (zero8,) * KRYLOV
@@ -164,6 +168,8 @@
         ).start()
     load_s.wait()
     load_w.wait()
+    load_p.wait()
+    load_t.wait()
     swap.wait()
     pltpu.make_async_copy(got1, got1, red_send.at[0]).wait()
     pltpu.make_async_copy(got2, got2, red_recv.at[1]).wait()
@@ -391,15 +397,16 @@
     vm = pltpu.VMEM
     dma = pltpu.SemaphoreType.DMA
     anywhere = pl.BlockSpec(memory_space=pltpu.HBM)
-    scalars = pl.BlockSpec(memory_space=pltpu.SMEM)
     return pl.pallas_call(
         kernel,
         out_shape=jax.ShapeDtypeStruct(adjoint.shape, f32),
-        in_specs=[anywhere] * 4 + [scalars] * 2,
+        in_specs=[anywhere] * 6,
         out_specs=pl.BlockSpec(memory_space=pltpu.VMEM),
         scratch_shapes=[
             vm(krylov.shape, krylov.dtype), vm(adjoint.shape, f32), vm(stencil.shape, stencil.dtype),
-            vm(column_weight.shape, f32), vm((PAIRS, ROWS, COLS), f32),
+            vm(column_weight.shape, f32),
+            pltpu.SMEM(projected.shape, f32), pltpu.SMEM(seam_turns.shape, jnp.int32),
+            vm((PAIRS, ROWS, COLS), f32),
             vm((KRYLOV, 2, HALF, COLS), f32), vm((KRYLOV, 2, HALF, COLS), f32),
             vm((KRYLOV, 2, HALF, COLS), f32),
             vm((CHUNKS, PART, COLS), f32), vm((CHUNKS, PART, COLS), f32), vm((CHUNKS, PART, COLS), f32),
@@ -409,14 +416,19 @@
             vm((len(GROUP_XY), 1, COLS), f32), vm((len(GROUP_ZC), 1, COLS), f32),
             vm((2, 16, COLS), f32), vm((2, 16, COLS), f32), vm((ROWS, COLS), f32), vm((COLS, COLS), f32),
             vm((2, 16, ROWS), f32), vm((2, 16, ROWS), f32), vm((2, COLS, COLS), f32), vm((ROWS, COLS), f32),
-            dma((2 * FIELDS + 2,)), dma((2,)), dma((2,)), dma((2,)), dma((2 * CHUNKS,)), dma((CHUNKS,)),
+            dma((2 * FIELDS + 4,)), dma((2,)), dma((2,)), dma((2,)), dma((2 * CHUNKS,)), dma((CHUNKS,)),
             dma((CHUNKS,)), dma((2 * CHUNKS,)), dma((8,)),
         ],
         name="step",
         compiler_params=pltpu.CompilerParams(
-            collective_id=0, has_side_effects=True, vmem_limit_bytes=60 << 20
+            collective_id=0, has_side_effects=True, vmem_limit_bytes=24 << 20
         ),
-    )(krylov, adjoint, stencil, column_weight, projected, seam_turns)
+    )(
+        *[
+            pltpu.with_memory_space_constraint(a, pltpu.HBM)
+            for a in (krylov, adjoint, stencil, column_weight, projected, seam_turns)
+        ]
+    )
 
 
 def solution(mesh):

time: 34.2 us -> 31 us (0.906)
  Pallas kernels: 31.6 us -> 29.8 us
  local copies, waits for them, and re-layouts: 2.47 us -> 1.06 us
    pallas_call x1, Pallas kernels: 31.6 us -> 29.8 us  [per_device(): pl.pallas_call(kernel, out_shape=jax.ShapeDtypeStruct(adjoint.shape, f32)...]
    unnamed x1, local copies, waits for them, and re-layouts: 2.47 us -> 1.06 us
where the time goes in v2:
time: 31 us; the launch traced here: 30.9 us
  Pallas kernels  29.8 us (96%)
  local copies, waits for them, and re-layouts  1.06 us (3%)
    pallas_call x1, Pallas kernels, per_device(): pl.pallas_call(kernel, out_shape=jax.ShapeDtypeStruct(adjoint.shape, f32)...  29.8 us
    unnamed x1, local copies, waits for them, and re-layouts  1.06 us

profile of v2, /device:TPU:1, one launch (start us, length us, event | category | flops | bytes accessed | tf_op | source)
XLA Modules:
  0.0 30.9 jit_solution(8222759877421109223)
XLA Ops:
  0.0 29.8 %step.1 = f32[2,5,256,128]{3,2,1,0:T(8,128)S(1)} custom-call(bf16[4,2,5,256,128]{4,3,2,1,0:T(8,128)(2,1)} %k_hbm.1, f32[2,5,256,128]{3,2,1,0:T(8,128)} %a_hbm.1, bf16[5,2,256,128]{3,2,1,0:T(8,128)(2,1)} %s_hbm.1, f32[2,2,256,128]{3,2,1,0:T(8,128)} %w_hbm.1, f32[4,4]{1,0:T(4,128)} %p_hbm.1, s32[1,4]{1,0:T(1,128)} %t_hbm.1), custom_call_target="tpu_custom_call" | custom-call | tf_op jit(solution)/shard_map/step/pallas_call | solution.py:400
  29.8 1.1 %copy.8 = f32[2,5,256,128]{3,2,1,0:T(8,128)} copy(f32[2,5,256,128]{3,2,1,0:T(8,128)S(1)} %step.1) | data formatting | bytes 2621440

commit v3 on v2

v3 whole, which is shorter than its diff:
```python
import jax
import jax.numpy as jnp
from jax import lax
from jax.experimental import pallas as pl
from jax.experimental.pallas import tpu as pltpu
from jax.sharding import PartitionSpec as P

MESH = pl.DeviceIdType.MESH
STRIDE = 4
KRYLOV = 4
FIELDS = 5
LEVELS = 2
ROWS = 256
COLS = 128
HALF = ROWS // 2
NX, NZ, NY, NC = 4, 8, 4, 2
PAIRS = LEVELS * FIELDS
STRIPS = KRYLOV * PAIRS
CHUNKS = 8
PART = 2 * HALF // CHUNKS
DIRECT = 2
RELAYED = CHUNKS - DIRECT
COUNT = 16 * FIELDS * 8192 * COLS


def ring(d, n):
    return min(d % n, (-d) % n)


GROUP_XY = sorted(
    [(dx, dy) for dx in range(NX) for dy in range(NY) if (dx, dy) != (0, 0)],
    key=lambda o: -(ring(o[0], NX) + ring(o[1], NY)),
)
GROUP_ZC = sorted(
    [(dz, dc) for dz in range(NZ) for dc in range(NC) if (dz, dc) != (0, 0)],
    key=lambda o: -(ring(o[0], NZ) + 0.5 * o[1]),
)


def splat_sum(x):
    return jnp.sum(jnp.sum(x, axis=0, keepdims=True), axis=1, keepdims=True)


def turned(strip, turn, lane_flip):
    odd = lax.rem(turn, 2) == 1
    cosine = jnp.where(turn == 0, 1.0, jnp.where(turn == 2, -1.0, 0.0)).astype(jnp.float32)
    sine = jnp.where(turn == 1, 1.0, jnp.where(turn == 3, -1.0, 0.0)).astype(jnp.float32)
    halves = [strip[:, i : i + COLS] for i in range(0, strip.shape[1], COLS)]
    back = [jnp.take_along_axis(h, lane_flip, axis=1) for h in halves[::-1]]
    field = lax.rem(lax.broadcasted_iota(jnp.int32, halves[0].shape, 0), FIELDS)
    out = []
    for h, b in zip(halves, back):
        x = jnp.where(odd, b, h)
        after = pltpu.roll(x, x.shape[0] - 1, 0)
        before = pltpu.roll(x, 1, 0)
        out.append(
            jnp.where(
                field == 2,
                cosine * x - sine * after,
                jnp.where(field == 3, sine * before + cosine * x, x),
            )
        )
    return out


def kernel(
    k_hbm, a_hbm, s_hbm, w_hbm, p_hbm, t_hbm,
    out,
    kv, av, sv, wv, proj, seam, coef, comb, pick, pick_coef,
    ls_own, ls_send, ls_recv, total, mine, relay, buf_a, buf_b, buf_c, below_send, below,
    row1, row2, got1, got2,
    row_send, row_got, row_mix, col_mix, col_t, col_send, col_got, strip_mix, col_back, col_add,
    load_sem, red_send, red_recv, swap_sem, y_send, a_sem, b_sem, c_sem, below_sem, edge_sem,
):
    t, l = lax.axis_index("tile"), lax.axis_index("lev")
    x, z, y, c = t // NZ, lax.rem(t, NZ), l // NC, lax.rem(l, NC)
    f32 = jnp.float32

    load_k = [pltpu.make_async_copy(k_hbm.at[:, :, f], kv.at[:, :, f], load_sem.at[f]) for f in range(FIELDS)]
    load_a = [pltpu.make_async_copy(a_hbm.at[:, f], av.at[:, f], load_sem.at[FIELDS + f]) for f in range(FIELDS)]
    load_s = pltpu.make_async_copy(s_hbm, sv, load_sem.at[2 * FIELDS])
    load_w = pltpu.make_async_copy(w_hbm, wv, load_sem.at[2 * FIELDS + 1])
    load_p = pltpu.make_async_copy(p_hbm, proj, load_sem.at[2 * FIELDS + 2])
    load_t = pltpu.make_async_copy(t_hbm, seam, load_sem.at[2 * FIELDS + 3])
    for f in range(FIELDS):
        load_k[f].start()
        load_a[f].start()

    def at_xy(dx, dy):
        return (lax.rem(x + dx, NX) * NZ + z, lax.rem(y + dy, NY) * NC + c)

    def at_zc(dz, dc):
        return (x * NZ + lax.rem(z + dz, NZ), y * NC + lax.rem(c + dc, NC))

    def at_tile(d):
        return (lax.rem(t + d + NX * NZ, NX * NZ), l)

    def remote(src, dst, send, recv, device):
        return pltpu.make_async_remote_copy(
            src_ref=src, dst_ref=dst, send_sem=send, recv_sem=recv, device_id=device, device_id_type=MESH
        )

    xy, zc = [at_xy(*o) for o in GROUP_XY], [at_zc(*o) for o in GROUP_ZC]
    core_peer, below_peer, above_peer = at_zc(0, 1), at_xy(0, NY - 1), at_xy(0, 1)
    edge_peers = [at_tile(d) for d in (1, -1, STRIDE, -STRIDE)]
    peers = edge_peers + xy + zc
    barrier = pltpu.get_barrier_semaphore()
    for peer in peers:
        pl.semaphore_signal(barrier, inc=1, device_id=peer, device_id_type=MESH)
    for load in (load_s, load_w, load_p, load_t):
        load.start()

    li = lax.broadcasted_iota(jnp.int32, (COLS, COLS), 0)
    lj = lax.broadcasted_iota(jnp.int32, (COLS, COLS), 1)

    def store_mask(ref, i, mask):
        ref[i] = jnp.where(mask, 1.0, 0.0).astype(jnp.bfloat16)

    for p in range(PAIRS):
        store_mask(pick, p, ((li == COLS - 1) & (lj == 2 * p)) | ((li == 0) & (lj == 2 * p + 1)))
    pair = lax.rem(lj, 2 * PAIRS)
    for lev in range(LEVELS):
        here = (pair >= 2 * FIELDS * lev) & (pair < 2 * FIELDS * (lev + 1)) & (lj < 2 * STRIPS)
        store_mask(pick_coef, lev, here & (li == COLS - 1) & (lax.rem(lj, 2) == 0))
        store_mask(pick_coef, LEVELS + lev, here & (li == 0) & (lax.rem(lj, 2) == 1))

    sums = (jnp.zeros((16, COLS), f32),) * KRYLOV
    for f in range(FIELDS):
        load_k[f].wait()
        load_a[f].wait()

        def dots(i, sums, f=f):
            lev, blk = i // 16, lax.rem(i, 16)
            at = pl.ds(pl.multiple_of(blk * 16, 16), 16)
            a = av[lev, f, at, :]
            return tuple(sums[k] + kv[k, lev, f, at, :].astype(f32) * a for k in range(KRYLOV))

        sums = lax.fori_loop(0, LEVELS * 16, dots, sums, unroll=4)

    lane1 = lax.broadcasted_iota(jnp.int32, (1, COLS), 1)
    mine_row = jnp.zeros((1, COLS), f32)
    for k in range(KRYLOV):
        mine_row = jnp.where(lane1 == k, splat_sum(sums[k]), mine_row)
    row1[...] = mine_row

    pl.semaphore_wait(barrier, len(peers))

    for j in range(len(xy)):
        remote(row1, got1.at[j], red_send.at[0], red_recv.at[0], xy[j]).start()

    keep, give = c * HALF, (1 - c) * HALF

    def swap(k):
        return remote(ls_send.at[k], ls_recv.at[k], swap_sem.at[0, k], swap_sem.at[1, k], core_peer)

    def level_sums(k, _):
        for g in range(2):
            for dst, start in ((ls_send, give), (ls_own, keep)):
                at = pl.ds(pl.multiple_of(start, HALF), HALF)
                dst[k, g] = kv[k, 0, 3 * g, at, :].astype(f32) + kv[k, 1, 3 * g, at, :].astype(f32)
        swap(k).start()
        return 0

    lax.fori_loop(0, KRYLOV, level_sums, 0)

    load_s.wait()
    parts = [sv[3, 0], sv[3, 1], sv[4, 0], sv[4, 1]]
    at_ends = sum(jnp.dot(parts[i], pick_coef[i], preferred_element_type=f32) for i in range(4))
    mixed = None
    for k in range(KRYLOV):
        strips = sum(
            jnp.dot(kv[k, p // FIELDS, p % FIELDS], pick[p], preferred_element_type=f32) for p in range(PAIRS)
        )
        strips = pltpu.roll(strips, 2 * PAIRS * k, 1) if k else strips
        mixed = strips if mixed is None else mixed + strips
    col_mix[...] = mixed * at_ends

    def edge_rows(k, _):
        for p in range(PAIRS):
            lev, f = p // FIELDS, p % FIELDS
            last = sv[1, lev, ROWS - 16 : ROWS, :].astype(f32) * kv[k, lev, f, ROWS - 16 : ROWS, :].astype(f32)
            first = sv[2, lev, 0:16, :].astype(f32) * kv[k, lev, f, 0:16, :].astype(f32)
            row_send[0, pl.ds(k * PAIRS + p, 1), :] = last[15:16]
            row_send[1, pl.ds(k * PAIRS + p, 1), :] = first[0:1]
        return 0

    lax.fori_loop(0, KRYLOV, edge_rows, 0)
    for i in range(2):
        col_t[...] = jnp.transpose(col_mix[i * COLS : (i + 1) * COLS, :])
        for s in range(2):
            col_send[s, :, i * COLS : (i + 1) * COLS] = col_t[pl.ds(s, STRIPS, stride=2), :]

    lane = lax.broadcasted_iota(jnp.int32, (ROWS, COLS), 1)
    row = lax.broadcasted_iota(jnp.int32, (ROWS, COLS), 0)
    for lev in range(LEVELS):
        coef[0, lev] = sv[0, lev].astype(f32)
        coef[1, lev] = jnp.where(row == ROWS - 1, 0.0, sv[1, lev].astype(f32))
        coef[2, lev] = jnp.where(row == 0, 0.0, sv[2, lev].astype(f32))
        coef[3, lev] = jnp.where(lane == COLS - 1, 0.0, sv[3, lev].astype(f32))
        coef[4, lev] = jnp.where(lane == 0, 0.0, sv[4, lev].astype(f32))

    pltpu.make_async_copy(got1, got1, red_recv.at[0]).wait()
    stage = row1[...]
    for j in range(len(xy)):
        stage = stage + got1[j]
    row2[...] = stage
    for j in range(len(zc)):
        remote(row2, got2.at[j], red_send.at[1], red_recv.at[1], zc[j]).start()

    edges = [
        remote(src, dst, edge_sem.at[s], edge_sem.at[4 + s], edge_peers[s])
        for s, (src, dst) in enumerate(
            (
                (row_send.at[0], row_got.at[0]),
                (row_send.at[1], row_got.at[1]),
                (col_send.at[0], col_got.at[0]),
                (col_send.at[1], col_got.at[1]),
            )
        )
    ]
    for s in (2, 3, 0, 1):
        edges[s].start()

    for k in range(KRYLOV):
        swap(k).wait()
        ls_send[k] = ls_own[k] + ls_recv[k]
    for load in (load_w, load_p, load_t):
        load.wait()
    pltpu.make_async_copy(got1, got1, red_send.at[0]).wait()

    pltpu.make_async_copy(got2, got2, red_recv.at[1]).wait()
    stage = row2[...]
    for j in range(len(zc)):
        stage = stage + got2[j]
    coupling = [
        jnp.sum(jnp.where(lane1 == k, stage, 0.0), axis=1, keepdims=True) * (0.5 / COUNT)
        for k in range(KRYLOV)
    ]
    mix, mix_one = [], []
    for j in range(KRYLOV):
        m = proj[0, j] * coupling[0]
        for k in range(1, KRYLOV):
            m = m + proj[k, j] * coupling[k]
        mix_one.append(m)
        mix.append(jnp.broadcast_to(m, (8, COLS)))

    def mixed(parts):
        acc = None
        for m, p in zip(mix, parts):
            term = jnp.concatenate([m] * (p.shape[0] // 8), axis=0) * p
            acc = term if acc is None else acc + term
        return acc

    def down(src, j):
        return remote(src.at[j], buf_a.at[j], y_send.at[0, j], a_sem.at[j], below_peer)

    def up(src, j):
        return remote(src.at[j], buf_b.at[j], y_send.at[1, j], b_sem.at[j], above_peer)

    def two_down(j):
        return remote(total.at[j], buf_c.at[j - RELAYED], y_send.at[2, j], c_sem.at[j - RELAYED], at_xy(0, 2))

    def two_up(j):
        return remote(total.at[j], buf_b.at[j], y_send.at[2, j], b_sem.at[j], at_xy(0, 2))

    for j in range(CHUNKS):
        g, at = (j * PART) // HALF, pl.ds((j * PART) % HALF, PART)
        total[j] = mixed([ls_send[k, g, at, :] for k in range(KRYLOV)])

        @pl.when(y == NY - 1)
        def _(j=j):
            if j >= RELAYED:
                two_up(j).start()
            down(total, j).start()
            up(total, j).start()

        @pl.when(y == 2)
        def _(j=j):
            if j >= RELAYED:
                two_down(j).start()
            down(total, j).start()

        if j >= RELAYED:

            @pl.when(y == 1)
            def _(j=j):
                down(total, j).start()

    for j in range(CHUNKS):
        g, at = (j * PART) // HALF, pl.ds((j * PART) % HALF, PART)
        mine[j] = mixed([ls_own[k, g, at, :] for k in range(KRYLOV)])

    @pl.when(y == NY - 1)
    def _():
        buf_a[...] = jnp.zeros(buf_a.shape, f32)

    @pl.when(y >= 2)
    def _():
        buf_b[...] = jnp.zeros(buf_b.shape, f32)

    @pl.when(y >= 1)
    def _():
        buf_c[...] = jnp.zeros(buf_c.shape, f32)

    def combine(i, _):
        lev, blk = i // 8, lax.rem(i, 8)
        at = pl.ds(pl.multiple_of(blk * 32, 32), 32)
        for f in range(FIELDS):
            comb[lev * FIELDS + f, at, :] = mixed([kv[k, lev, f, at, :].astype(f32) for k in range(KRYLOV)])
        return 0

    lax.fori_loop(0, LEVELS * 8, combine, 0)

    outer = (lane == 0) | (lane == COLS - 1)

    def interior(p, _):
        lev, f = p // FIELDS, lax.rem(p, FIELDS)
        field = comb[p]
        acc = av[lev, f] + jnp.where(outer, pltpu.roll(col_add[...], COLS - 1 - 2 * p, 1), 0.0)
        acc = acc + coef[0, lev] * field
        acc = acc + pltpu.roll(coef[1, lev] * field, 1, 0)
        acc = acc + pltpu.roll(coef[2, lev] * field, ROWS - 1, 0)
        acc = acc + pltpu.roll(coef[3, lev] * field, 1, 1)
        acc = acc + pltpu.roll(coef[4, lev] * field, COLS - 1, 1)
        out[lev, f] = acc
        out[lev, f, 0:1, :] = acc[0:1] + row_mix[0, pl.ds(p, 1), :]
        out[lev, f, ROWS - 1 : ROWS, :] = acc[ROWS - 1 : ROWS] + row_mix[1, pl.ds(p, 1), :]
        return 0

    def pass_on(j, _):
        @pl.when(y == 1)
        def _():
            down(total, j).wait_recv()
            relay[j] = total[j] + buf_a[j]
            down(relay, j).start()

        @pl.when(y == 0)
        def _():
            up(total, j).wait_recv()
            up(buf_b, j).start()

        return 0

    lax.fori_loop(0, RELAYED // 2, pass_on, 0)

    for s in range(4):
        edges[s].wait()

    def mixed_strips(ref, s):
        return sum(mix_one[k] * ref[s, k * PAIRS : (k + 1) * PAIRS, :] for k in range(KRYLOV))

    lane_flip = COLS - 1 - lax.broadcasted_iota(jnp.int32, (16, COLS), 1)
    for s in range(2):
        row_mix[s, 0:PAIRS, :] = mixed_strips(row_got, s)
        strip_mix[s, 0:PAIRS, :] = mixed_strips(col_got, s)
    for s in range(2):
        row_mix[s] = turned(row_mix[s], seam[0, s], lane_flip)[0]
        parts = turned(strip_mix[s], seam[0, 2 + s], lane_flip)
        for i in range(2):
            col_back[i, pl.ds(1 - s, 16, stride=2), :] = parts[i]
    col_add[0:COLS, :] = jnp.transpose(col_back[0])
    col_add[COLS:ROWS, :] = jnp.transpose(col_back[1])

    def pass_and_interior(j, _):
        pass_on(RELAYED // 2 + j, 0)
        steps = RELAYED - RELAYED // 2
        lax.fori_loop(j * PAIRS // steps, (j + 1) * PAIRS // steps, interior, 0)
        return 0

    lax.fori_loop(0, RELAYED - RELAYED // 2, pass_and_interior, 0)

    def hand(j):
        return remote(below_send.at[j], below.at[j], below_sem.at[0, j], below_sem.at[1, j], core_peer)

    def integrals(j, start, sums):
        g = (j * PART) // HALF
        at = pl.ds(pl.multiple_of(start + lax.rem(j * PART, HALF), PART), PART)
        upper = sums + comb[FIELDS + 3 * g, at, :]
        lower = upper + comb[3 * g, at, :]
        f = 1 + 3 * g
        out[1, f, at, :] = out[1, f, at, :] + wv[g, 1, at, :] * upper
        out[0, f, at, :] = out[0, f, at, :] + wv[g, 0, at, :] * lower

    def finish_mine(j, _, direct=False):
        @pl.when((y == 2) | (y == 0))
        def _():
            down(total, j).wait_recv()

        @pl.when(y == 1)
        def _():
            up(total, j).wait_recv()
            if direct:
                down(total, j).wait_recv()

        if direct:

            @pl.when(y == 0)
            def _():
                up(total, j).wait_recv()
                two_down(j).wait_recv()

        higher = buf_a[j] + buf_b[j]
        if direct:
            higher = higher + buf_c[j - RELAYED]
        below_send[j] = jnp.where(c == 1, higher + mine[j], higher)
        hand(j).start()
        integrals(j, keep, jnp.where(c == 1, higher, higher + (total[j] - mine[j])))
        return 0

    def finish_other(j, _):
        hand(j).wait()
        integrals(j, give, below[j])
        return 0

    lax.fori_loop(0, RELAYED, finish_mine, 0)
    lax.fori_loop(RELAYED, CHUNKS, lambda j, _: finish_mine(j, 0, True), 0)

    def sent(j, _, direct=False):
        @pl.when(y >= 1)
        def _():
            down(total, j).wait_send()

        @pl.when((y == NY - 1) if direct else ((y == NY - 1) | (y == 0)))
        def _():
            up(total, j).wait_send()

        if direct:

            @pl.when(y >= 2)
            def _():
                two_down(j).wait_send()

        return 0

    lax.fori_loop(0, RELAYED, sent, 0)
    lax.fori_loop(RELAYED, CHUNKS, lambda j, _: sent(j, 0, True), 0)
    pltpu.make_async_copy(got2, got2, red_send.at[1]).wait()
    lax.fori_loop(0, CHUNKS, finish_other, 0)


def per_device(krylov, adjoint, projected, stencil, column_weight, seam_turns):
    f32 = jnp.float32
    vm = pltpu.VMEM
    dma = pltpu.SemaphoreType.DMA
    part = vm((CHUNKS, PART, COLS), f32)
    sums = vm((KRYLOV, 2, HALF, COLS), f32)
    return pl.pallas_call(
        kernel,
        out_shape=jax.ShapeDtypeStruct(adjoint.shape, f32),
        in_specs=[pl.BlockSpec(memory_space=pltpu.HBM)] * 6,
        out_specs=pl.BlockSpec(memory_space=pltpu.VMEM),
        scratch_shapes=[
            vm(krylov.shape, krylov.dtype), vm(adjoint.shape, f32), vm(stencil.shape, stencil.dtype),
            vm(column_weight.shape, f32),
            pltpu.SMEM(projected.shape, f32), pltpu.SMEM(seam_turns.shape, jnp.int32),
            vm(stencil.shape, f32), vm((PAIRS, ROWS, COLS), f32),
            vm((PAIRS, COLS, COLS), jnp.bfloat16), vm((2 * LEVELS, COLS, COLS), jnp.bfloat16),
            sums, sums, sums, part, part, part, part, part, vm((max(DIRECT, 1), PART, COLS), f32), part, part,
            vm((1, COLS), f32), vm((1, COLS), f32),
            vm((len(GROUP_XY), 1, COLS), f32), vm((len(GROUP_ZC), 1, COLS), f32),
            vm((2, STRIPS, COLS), f32), vm((2, STRIPS, COLS), f32), vm((2, 16, COLS), f32), vm((ROWS, COLS), f32),
            vm((COLS, COLS), f32), vm((2, STRIPS, ROWS), f32), vm((2, STRIPS, ROWS), f32), vm((2, 16, ROWS), f32),
            vm((2, COLS, COLS), f32), vm((ROWS, COLS), f32),
            dma((2 * FIELDS + 4,)), dma((2,)), dma((2,)), dma((2, KRYLOV)), dma((3, CHUNKS)), dma((CHUNKS,)),
            dma((CHUNKS,)), dma((max(DIRECT, 1),)), dma((2, CHUNKS)), dma((8,)),
        ],
        name="step",
        compiler_params=pltpu.CompilerParams(
            collective_id=0, has_side_effects=True, vmem_limit_bytes=32 << 20
        ),
    )(
        *[
            pltpu.with_memory_space_constraint(a, pltpu.HBM)
            for a in (krylov, adjoint, stencil, column_weight, projected, seam_turns)
        ]
    )


def solution(mesh):
    placed = (
        P(None, "lev", None, "tile", None),
        P("lev", None, "tile", None),
        P(),
        P(None, "lev", "tile", None),
        P(None, "lev", "tile", None),
        P("tile", None),
    )
    return jax.shard_map(
        per_device,
        mesh=mesh,
        in_specs=placed,
        out_specs=P("lev", None, "tile", None),
        check_vma=False,
    )
```

time: 31 us -> 30.1 us (0.971)
  Pallas kernels: 29.8 us -> 29 us
    pallas_call x1, Pallas kernels: 29.8 us -> 29 us  [per_device(): pl.pallas_call(kernel, out_shape=jax.ShapeDtypeStruct(adjoint.shape, f32)...]
where the time goes in v3:
time: 30.1 us; the launch traced here: 30 us
  Pallas kernels  29 us (96%)
  local copies, waits for them, and re-layouts  1.06 us (4%)
    pallas_call x1, Pallas kernels, per_device(): pl.pallas_call(kernel, out_shape=jax.ShapeDtypeStruct(adjoint.shape, f32)...  29 us
    unnamed x1, local copies, waits for them, and re-layouts  1.06 us

profile of v3, /device:TPU:1, one launch (start us, length us, event | category | flops | bytes accessed | tf_op | source)
XLA Modules:
  0.0 30.0 jit_solution(1209541494902473994)
XLA Ops:
  0.0 29.0 %step.1 = f32[2,5,256,128]{3,2,1,0:T(8,128)S(1)} custom-call(bf16[4,2,5,256,128]{4,3,2,1,0:T(8,128)(2,1)} %k_hbm.1, f32[2,5,256,128]{3,2,1,0:T(8,128)} %a_hbm.1, bf16[5,2,256,128]{3,2,1,0:T(8,128)(2,1)} %s_hbm.1, f32[2,2,256,128]{3,2,1,0:T(8,128)} %w_hbm.1, f32[4,4]{1,0:T(4,128)} %p_hbm.1, s32[1,4]{1,0:T(1,128)} %t_hbm.1), custom_call_target="tpu_custom_call" | custom-call | tf_op jit(solution)/shard_map/step/pallas_call | solution.py:447
  29.0 1.1 %copy.8 = f32[2,5,256,128]{3,2,1,0:T(8,128)} copy(f32[2,5,256,128]{3,2,1,0:T(8,128)S(1)} %step.1) | data formatting | bytes 2621440

commit v4 on v3

--- a/solution.py
+++ b/solution.py
@@ -18,8 +18,8 @@
 STRIPS = KRYLOV * PAIRS
 CHUNKS = 8
 PART = 2 * HALF // CHUNKS
-DIRECT = 2
-RELAYED = CHUNKS - DIRECT
+EARLY = 4
+EARLIEST = 1
 COUNT = 16 * FIELDS * 8192 * COLS
 
 
@@ -27,14 +27,18 @@
     return min(d % n, (-d) % n)
 
 
-GROUP_XY = sorted(
-    [(dx, dy) for dx in range(NX) for dy in range(NY) if (dx, dy) != (0, 0)],
-    key=lambda o: -(ring(o[0], NX) + ring(o[1], NY)),
-)
-GROUP_ZC = sorted(
-    [(dz, dc) for dz in range(NZ) for dc in range(NC) if (dz, dc) != (0, 0)],
-    key=lambda o: -(ring(o[0], NZ) + 0.5 * o[1]),
-)
+def group(nx, nz, ny, nc):
+    offsets = [
+        (dx, dz, dy, dc) for dx in range(nx) for dz in range(nz) for dy in range(ny) for dc in range(nc)
+    ]
+    return sorted(
+        offsets[1:], key=lambda o: -(ring(o[0], NX) + ring(o[1], NZ) + ring(o[2], NY) + 0.5 * o[3])
+    )
+
+
+FIRST = group(NX, 1, NY, 1)
+SECOND = group(1, NZ, 1, NC)
+UNROLL = 16
 
 
 def splat_sum(x):
@@ -67,10 +71,10 @@
     k_hbm, a_hbm, s_hbm, w_hbm, p_hbm, t_hbm,
     out,
     kv, av, sv, wv, proj, seam, coef, comb, pick, pick_coef,
-    ls_own, ls_send, ls_recv, total, mine, relay, buf_a, buf_b, buf_c, below_send, below,
+    ls_own, ls_send, ls_recv, total, mine, relay, buf_a, buf_b, raw_a, raw_b, below_send, below,
     row1, row2, got1, got2,
     row_send, row_got, row_mix, col_mix, col_t, col_send, col_got, strip_mix, col_back, col_add,
-    load_sem, red_send, red_recv, swap_sem, y_send, a_sem, b_sem, c_sem, below_sem, edge_sem,
+    load_sem, red_send, red_recv, swap_sem, y_send, a_sem, b_sem, raw_send, raw_a_sem, raw_b_sem, below_sem, edge_sem,
 ):
     t, l = lax.axis_index("tile"), lax.axis_index("lev")
     x, z, y, c = t // NZ, lax.rem(t, NZ), l // NC, lax.rem(l, NC)
@@ -86,24 +90,23 @@
         load_k[f].start()
         load_a[f].start()
 
-    def at_xy(dx, dy):
-        return (lax.rem(x + dx, NX) * NZ + z, lax.rem(y + dy, NY) * NC + c)
-
-    def at_zc(dz, dc):
-        return (x * NZ + lax.rem(z + dz, NZ), y * NC + lax.rem(c + dc, NC))
+    def device(dx, dz, dy, dc):
+        return (
+            lax.rem(x + dx, NX) * NZ + lax.rem(z + dz, NZ), lax.rem(y + dy, NY) * NC + lax.rem(c + dc, NC)
+        )
 
     def at_tile(d):
         return (lax.rem(t + d + NX * NZ, NX * NZ), l)
 
-    def remote(src, dst, send, recv, device):
+    def remote(src, dst, send, recv, where):
         return pltpu.make_async_remote_copy(
-            src_ref=src, dst_ref=dst, send_sem=send, recv_sem=recv, device_id=device, device_id_type=MESH
+            src_ref=src, dst_ref=dst, send_sem=send, recv_sem=recv, device_id=where, device_id_type=MESH
         )
 
-    xy, zc = [at_xy(*o) for o in GROUP_XY], [at_zc(*o) for o in GROUP_ZC]
-    core_peer, below_peer, above_peer = at_zc(0, 1), at_xy(0, NY - 1), at_xy(0, 1)
+    first, second = [device(*o) for o in FIRST], [device(*o) for o in SECOND]
+    core_peer, below_peer, above_peer = device(0, 0, 0, 1), device(0, 0, NY - 1, 0), device(0, 0, 1, 0)
     edge_peers = [at_tile(d) for d in (1, -1, STRIDE, -STRIDE)]
-    peers = edge_peers + xy + zc
+    peers = edge_peers + first + second
     barrier = pltpu.get_barrier_semaphore()
     for peer in peers:
         pl.semaphore_signal(barrier, inc=1, device_id=peer, device_id_type=MESH)
@@ -135,7 +138,7 @@
             a = av[lev, f, at, :]
             return tuple(sums[k] + kv[k, lev, f, at, :].astype(f32) * a for k in range(KRYLOV))
 
-        sums = lax.fori_loop(0, LEVELS * 16, dots, sums, unroll=4)
+        sums = lax.fori_loop(0, LEVELS * 16, dots, sums, unroll=UNROLL)
 
     lane1 = lax.broadcasted_iota(jnp.int32, (1, COLS), 1)
     mine_row = jnp.zeros((1, COLS), f32)
@@ -145,8 +148,8 @@
 
     pl.semaphore_wait(barrier, len(peers))
 
-    for j in range(len(xy)):
-        remote(row1, got1.at[j], red_send.at[0], red_recv.at[0], xy[j]).start()
+    for j in range(len(first)):
+        remote(row1, got1.at[j], red_send.at[0], red_recv.at[0], first[j]).start()
 
     keep, give = c * HALF, (1 - c) * HALF
 
@@ -199,13 +202,40 @@
         coef[3, lev] = jnp.where(lane == COLS - 1, 0.0, sv[3, lev].astype(f32))
         coef[4, lev] = jnp.where(lane == 0, 0.0, sv[4, lev].astype(f32))
 
+    for k in range(KRYLOV):
+        swap(k).wait()
+        ls_send[k] = ls_own[k] + ls_recv[k]
+
+    def span(j):
+        return (j * PART) // HALF, pl.ds((j * PART) % HALF, PART)
+
+    def raw_down(j):
+        g, rows = span(j)
+        return remote(ls_send.at[:, g, rows], raw_a.at[j], raw_send.at[0, j], raw_a_sem.at[j], below_peer)
+
+    def raw_up(j):
+        g, rows = span(j)
+        return remote(ls_send.at[:, g, rows], raw_b.at[j], raw_send.at[1, j], raw_b_sem.at[j], above_peer)
+
+    def send_raw(j):
+        @pl.when(y >= 2)
+        def _():
+            raw_down(j).start()
+
+        @pl.when(y == NY - 1)
+        def _():
+            raw_up(j).start()
+
+    for j in range(EARLIEST):
+        send_raw(j)
+
     pltpu.make_async_copy(got1, got1, red_recv.at[0]).wait()
     stage = row1[...]
-    for j in range(len(xy)):
+    for j in range(len(first)):
         stage = stage + got1[j]
     row2[...] = stage
-    for j in range(len(zc)):
-        remote(row2, got2.at[j], red_send.at[1], red_recv.at[1], zc[j]).start()
+    for j in range(len(second)):
+        remote(row2, got2.at[j], red_send.at[1], red_recv.at[1], second[j]).start()
 
     edges = [
         remote(src, dst, edge_sem.at[s], edge_sem.at[4 + s], edge_peers[s])
@@ -221,16 +251,15 @@
     for s in (2, 3, 0, 1):
         edges[s].start()
 
-    for k in range(KRYLOV):
-        swap(k).wait()
-        ls_send[k] = ls_own[k] + ls_recv[k]
+    for j in range(EARLIEST, EARLY):
+        send_raw(j)
     for load in (load_w, load_p, load_t):
         load.wait()
     pltpu.make_async_copy(got1, got1, red_send.at[0]).wait()
 
     pltpu.make_async_copy(got2, got2, red_recv.at[1]).wait()
     stage = row2[...]
-    for j in range(len(zc)):
+    for j in range(len(second)):
         stage = stage + got2[j]
     coupling = [
         jnp.sum(jnp.where(lane1 == k, stage, 0.0), axis=1, keepdims=True) * (0.5 / COUNT)
@@ -257,38 +286,47 @@
     def up(src, j):
         return remote(src.at[j], buf_b.at[j], y_send.at[1, j], b_sem.at[j], above_peer)
 
-    def two_down(j):
-        return remote(total.at[j], buf_c.at[j - RELAYED], y_send.at[2, j], c_sem.at[j - RELAYED], at_xy(0, 2))
-
-    def two_up(j):
-        return remote(total.at[j], buf_b.at[j], y_send.at[2, j], b_sem.at[j], at_xy(0, 2))
+    for j in range(EARLY, CHUNKS):
+        g, rows = span(j)
+        total[j] = mixed([ls_send[k, g, rows, :] for k in range(KRYLOV)])
+
+        @pl.when(y >= 2)
+        def _(j=j):
+            down(total, j).start()
+
+        @pl.when(y == NY - 1)
+        def _(j=j):
+            up(total, j).start()
+
+    def pass_down(j):
+        return remote(relay.at[j], buf_b.at[j], y_send.at[0, j], b_sem.at[j], below_peer)
+
+    for j in range(EARLY):
+        g, rows = span(j)
+        total[j] = mixed([ls_send[k, g, rows, :] for k in range(KRYLOV)])
+
+        @pl.when(y == 2)
+        def _(j=j):
+            raw_down(j).wait_recv()
+            relay[j] = mixed([raw_a[j, k] for k in range(KRYLOV)])
+            pass_down(j).start()
+            buf_a[j] = relay[j]
+
+        @pl.when(y == 1)
+        def _(j=j):
+            raw_down(j).wait_recv()
+            buf_a[j] = mixed([raw_a[j, k] for k in range(KRYLOV)])
+            relay[j] = total[j] + buf_a[j]
+            down(relay, j).start()
+
+        @pl.when(y == 0)
+        def _(j=j):
+            raw_up(j).wait_recv()
+            buf_b[j] = mixed([raw_b[j, k] for k in range(KRYLOV)])
 
     for j in range(CHUNKS):
-        g, at = (j * PART) // HALF, pl.ds((j * PART) % HALF, PART)
-        total[j] = mixed([ls_send[k, g, at, :] for k in range(KRYLOV)])
-
-        @pl.when(y == NY - 1)
-        def _(j=j):
-            if j >= RELAYED:
-                two_up(j).start()
-            down(total, j).start()
-            up(total, j).start()
-
-        @pl.when(y == 2)
-        def _(j=j):
-            if j >= RELAYED:
-                two_down(j).start()
-            down(total, j).start()
-
-        if j >= RELAYED:
-
-            @pl.when(y == 1)
-            def _(j=j):
-                down(total, j).start()
-
-    for j in range(CHUNKS):
-        g, at = (j * PART) // HALF, pl.ds((j * PART) % HALF, PART)
-        mine[j] = mixed([ls_own[k, g, at, :] for k in range(KRYLOV)])
+        g, rows = span(j)
+        mine[j] = mixed([ls_own[k, g, rows, :] for k in range(KRYLOV)])
 
     @pl.when(y == NY - 1)
     def _():
@@ -297,10 +335,6 @@
     @pl.when(y >= 2)
     def _():
         buf_b[...] = jnp.zeros(buf_b.shape, f32)
-
-    @pl.when(y >= 1)
-    def _():
-        buf_c[...] = jnp.zeros(buf_c.shape, f32)
 
     def combine(i, _):
         lev, blk = i // 8, lax.rem(i, 8)
@@ -341,7 +375,7 @@
 
         return 0
 
-    lax.fori_loop(0, RELAYED // 2, pass_on, 0)
+    lax.fori_loop(EARLY, EARLY + 2, pass_on, 0)
 
     for s in range(4):
         edges[s].wait()
@@ -362,12 +396,12 @@
     col_add[COLS:ROWS, :] = jnp.transpose(col_back[1])
 
     def pass_and_interior(j, _):
-        pass_on(RELAYED // 2 + j, 0)
-        steps = RELAYED - RELAYED // 2
+        pass_on(EARLY + 2 + j, 0)
+        steps = CHUNKS - EARLY - 2
         lax.fori_loop(j * PAIRS // steps, (j + 1) * PAIRS // steps, interior, 0)
         return 0
 
-    lax.fori_loop(0, RELAYED - RELAYED // 2, pass_and_interior, 0)
+    lax.fori_loop(0, CHUNKS - EARLY - 2, pass_and_interior, 0)
 
     def hand(j):
         return remote(below_send.at[j], below.at[j], below_sem.at[0, j], below_sem.at[1, j], core_peer)
@@ -381,27 +415,16 @@
         out[1, f, at, :] = out[1, f, at, :] + wv[g, 1, at, :] * upper
         out[0, f, at, :] = out[0, f, at, :] + wv[g, 0, at, :] * lower
 
-    def finish_mine(j, _, direct=False):
-        @pl.when((y == 2) | (y == 0))
+    def finish_mine(j, _, early=False):
+        @pl.when((y == 0) if early else ((y == 2) | (y == 0)))
         def _():
             down(total, j).wait_recv()
 
         @pl.when(y == 1)
         def _():
             up(total, j).wait_recv()
-            if direct:
-                down(total, j).wait_recv()
-
-        if direct:
-
-            @pl.when(y == 0)
-            def _():
-                up(total, j).wait_recv()
-                two_down(j).wait_recv()
 
         higher = buf_a[j] + buf_b[j]
-        if direct:
-            higher = higher + buf_c[j - RELAYED]
         below_send[j] = jnp.where(c == 1, higher + mine[j], higher)
         hand(j).start()
         integrals(j, keep, jnp.where(c == 1, higher, higher + (total[j] - mine[j])))
@@ -412,28 +435,34 @@
         integrals(j, give, below[j])
         return 0
 
-    lax.fori_loop(0, RELAYED, finish_mine, 0)
-    lax.fori_loop(RELAYED, CHUNKS, lambda j, _: finish_mine(j, 0, True), 0)
-
-    def sent(j, _, direct=False):
-        @pl.when(y >= 1)
+    lax.fori_loop(0, EARLY, lambda j, _: finish_mine(j, 0, True), 0)
+    lax.fori_loop(EARLY, CHUNKS, finish_mine, 0)
+
+    def sent(j, _, early=False):
+        @pl.when(((y == 1) | (y == 2)) if early else (y >= 1))
         def _():
             down(total, j).wait_send()
 
-        @pl.when((y == NY - 1) if direct else ((y == NY - 1) | (y == 0)))
-        def _():
-            up(total, j).wait_send()
-
-        if direct:
-
-            @pl.when(y >= 2)
+        if not early:
+
+            @pl.when((y == NY - 1) | (y == 0))
             def _():
-                two_down(j).wait_send()
-
-        return 0
-
-    lax.fori_loop(0, RELAYED, sent, 0)
-    lax.fori_loop(RELAYED, CHUNKS, lambda j, _: sent(j, 0, True), 0)
+                up(total, j).wait_send()
+
+        return 0
+
+    for j in range(EARLY):
+
+        @pl.when(y >= 2)
+        def _(j=j):
+            raw_down(j).wait_send()
+
+        @pl.when(y == NY - 1)
+        def _(j=j):
+            raw_up(j).wait_send()
+
+    lax.fori_loop(0, EARLY, lambda j, _: sent(j, 0, True), 0)
+    lax.fori_loop(EARLY, CHUNKS, sent, 0)
     pltpu.make_async_copy(got2, got2, red_send.at[1]).wait()
     lax.fori_loop(0, CHUNKS, finish_other, 0)
 
@@ -443,6 +472,7 @@
     vm = pltpu.VMEM
     dma = pltpu.SemaphoreType.DMA
     part = vm((CHUNKS, PART, COLS), f32)
+    raw = vm((EARLY, KRYLOV, PART, COLS), f32)
     sums = vm((KRYLOV, 2, HALF, COLS), f32)
     return pl.pallas_call(
         kernel,
@@ -455,14 +485,14 @@
             pltpu.SMEM(projected.shape, f32), pltpu.SMEM(seam_turns.shape, jnp.int32),
             vm(stencil.shape, f32), vm((PAIRS, ROWS, COLS), f32),
             vm((PAIRS, COLS, COLS), jnp.bfloat16), vm((2 * LEVELS, COLS, COLS), jnp.bfloat16),
-            sums, sums, sums, part, part, part, part, part, vm((max(DIRECT, 1), PART, COLS), f32), part, part,
+            sums, sums, sums, part, part, part, part, part, raw, raw, part, part,
             vm((1, COLS), f32), vm((1, COLS), f32),
-            vm((len(GROUP_XY), 1, COLS), f32), vm((len(GROUP_ZC), 1, COLS), f32),
+            vm((len(FIRST), 1, COLS), f32), vm((len(SECOND), 1, COLS), f32),
             vm((2, STRIPS, COLS), f32), vm((2, STRIPS, COLS), f32), vm((2, 16, COLS), f32), vm((ROWS, COLS), f32),
             vm((COLS, COLS), f32), vm((2, STRIPS, ROWS), f32), vm((2, STRIPS, ROWS), f32), vm((2, 16, ROWS), f32),
             vm((2, COLS, COLS), f32), vm((ROWS, COLS), f32),
-            dma((2 * FIELDS + 4,)), dma((2,)), dma((2,)), dma((2, KRYLOV)), dma((3, CHUNKS)), dma((CHUNKS,)),
-            dma((CHUNKS,)), dma((max(DIRECT, 1),)), dma((2, CHUNKS)), dma((8,)),
+            dma((2 * FIELDS + 4,)), dma((2,)), dma((2,)), dma((2, KRYLOV)), dma((2, CHUNKS)), dma((CHUNKS,)),
+            dma((CHUNKS,)), dma((2, EARLY)), dma((EARLY,)), dma((EARLY,)), dma((2, CHUNKS)), dma((8,)),
         ],
         name="step",
         compiler_params=pltpu.CompilerParams(

time: 30.1 us -> 29.6 us (0.983)
  Pallas kernels: 29 us -> 28.4 us
    pallas_call x1, Pallas kernels: 29 us -> 28.4 us  [per_device(): pl.pallas_call(kernel, out_shape=jax.ShapeDtypeStruct(adjoint.shape, f32)...]
where the time goes in v4:
time: 29.6 us; the launch traced here: 29.5 us
  Pallas kernels  28.4 us (96%)
  local copies, waits for them, and re-layouts  1.06 us (4%)
    pallas_call x1, Pallas kernels, per_device(): pl.pallas_call(kernel, out_shape=jax.ShapeDtypeStruct(adjoint.shape, f32)...  28.4 us
    unnamed x1, local copies, waits for them, and re-layouts  1.06 us

profile of v4, /device:TPU:1, one launch (start us, length us, event | category | flops | bytes accessed | tf_op | source)
XLA Modules:
  0.0 29.5 jit_solution(2255607987334853573)
XLA Ops:
  0.0 28.4 %step.1 = f32[2,5,256,128]{3,2,1,0:T(8,128)S(1)} custom-call(bf16[4,2,5,256,128]{4,3,2,1,0:T(8,128)(2,1)} %k_hbm.1, f32[2,5,256,128]{3,2,1,0:T(8,128)} %a_hbm.1, bf16[5,2,256,128]{3,2,1,0:T(8,128)(2,1)} %s_hbm.1, f32[2,2,256,128]{3,2,1,0:T(8,128)} %w_hbm.1, f32[4,4]{1,0:T(4,128)} %p_hbm.1, s32[1,4]{1,0:T(1,128)} %t_hbm.1), custom_call_target="tpu_custom_call" | custom-call | tf_op jit(solution)/shard_map/step/pallas_call | solution.py:477
  28.4 1.1 %copy.8 = f32[2,5,256,128]{3,2,1,0:T(8,128)} copy(f32[2,5,256,128]{3,2,1,0:T(8,128)S(1)} %step.1) | data formatting | bytes 2621440

commit v5 on v4

--- a/solution.py
+++ b/solution.py
@@ -106,7 +106,7 @@
     first, second = [device(*o) for o in FIRST], [device(*o) for o in SECOND]
     core_peer, below_peer, above_peer = device(0, 0, 0, 1), device(0, 0, NY - 1, 0), device(0, 0, 1, 0)
     edge_peers = [at_tile(d) for d in (1, -1, STRIDE, -STRIDE)]
-    peers = edge_peers + first + second
+    peers = second + first + edge_peers
     barrier = pltpu.get_barrier_semaphore()
     for peer in peers:
         pl.semaphore_signal(barrier, inc=1, device_id=peer, device_id_type=MESH)
@@ -375,7 +375,7 @@
 
         return 0
 
-    lax.fori_loop(EARLY, EARLY + 2, pass_on, 0)
+    lax.fori_loop(EARLY, CHUNKS, pass_on, 0)
 
     for s in range(4):
         edges[s].wait()
@@ -395,13 +395,7 @@
     col_add[0:COLS, :] = jnp.transpose(col_back[0])
     col_add[COLS:ROWS, :] = jnp.transpose(col_back[1])
 
-    def pass_and_interior(j, _):
-        pass_on(EARLY + 2 + j, 0)
-        steps = CHUNKS - EARLY - 2
-        lax.fori_loop(j * PAIRS // steps, (j + 1) * PAIRS // steps, interior, 0)
-        return 0
-
-    lax.fori_loop(0, CHUNKS - EARLY - 2, pass_and_interior, 0)
+    lax.fori_loop(0, PAIRS, interior, 0)
 
     def hand(j):
         return remote(below_send.at[j], below.at[j], below_sem.at[0, j], below_sem.at[1, j], core_peer)

time: 29.6 us -> 29.2 us (0.986)
  Pallas kernels: 28.4 us -> 28 us
    pallas_call x1, Pallas kernels: 28.4 us -> 28 us  [per_device(): pl.pallas_call(kernel, out_shape=jax.ShapeDtypeStruct(adjoint.shape, f32)...]
where the time goes in v5:
time: 29.2 us; the launch traced here: 29.1 us
  Pallas kernels  28 us (96%)
  local copies, waits for them, and re-layouts  1.06 us (4%)
    pallas_call x1, Pallas kernels, per_device(): pl.pallas_call(kernel, out_shape=jax.ShapeDtypeStruct(adjoint.shape, f32)...  28 us
    unnamed x1, local copies, waits for them, and re-layouts  1.06 us

profile of v5, /device:TPU:1, one launch (start us, length us, event | category | flops | bytes accessed | tf_op | source)
XLA Modules:
  0.0 29.1 jit_solution(388152075518523713)
XLA Ops:
  0.0 28.0 %step.1 = f32[2,5,256,128]{3,2,1,0:T(8,128)S(1)} custom-call(bf16[4,2,5,256,128]{4,3,2,1,0:T(8,128)(2,1)} %k_hbm.1, f32[2,5,256,128]{3,2,1,0:T(8,128)} %a_hbm.1, bf16[5,2,256,128]{3,2,1,0:T(8,128)(2,1)} %s_hbm.1, f32[2,2,256,128]{3,2,1,0:T(8,128)} %w_hbm.1, f32[4,4]{1,0:T(4,128)} %p_hbm.1, s32[1,4]{1,0:T(1,128)} %t_hbm.1), custom_call_target="tpu_custom_call" | custom-call | tf_op jit(solution)/shard_map/step/pallas_call | solution.py:471
  28.0 1.1 %copy.8 = f32[2,5,256,128]{3,2,1,0:T(8,128)} copy(f32[2,5,256,128]{3,2,1,0:T(8,128)S(1)} %step.1) | data formatting | bytes 2621440

commit v6 on v5

--- a/solution.py
+++ b/solution.py
@@ -106,7 +106,7 @@
     first, second = [device(*o) for o in FIRST], [device(*o) for o in SECOND]
     core_peer, below_peer, above_peer = device(0, 0, 0, 1), device(0, 0, NY - 1, 0), device(0, 0, 1, 0)
     edge_peers = [at_tile(d) for d in (1, -1, STRIDE, -STRIDE)]
-    peers = second + first + edge_peers
+    peers = second + first
     barrier = pltpu.get_barrier_semaphore()
     for peer in peers:
         pl.semaphore_signal(barrier, inc=1, device_id=peer, device_id_type=MESH)

time: 29.2 us -> 29 us (level)
  no operation moved by 1% of the time
where the time goes in v6:
time: 29 us; the launch traced here: 28.9 us
  Pallas kernels  27.9 us (96%)
  local copies, waits for them, and re-layouts  1.06 us (4%)
    pallas_call x1, Pallas kernels, per_device(): pl.pallas_call(kernel, out_shape=jax.ShapeDtypeStruct(adjoint.shape, f32)...  27.9 us
    unnamed x1, local copies, waits for them, and re-layouts  1.06 us

profile of v6, /device:TPU:1, one launch (start us, length us, event | category | flops | bytes accessed | tf_op | source)
XLA Modules:
  0.0 28.9 jit_solution(16274761639186150794)
XLA Ops:
  0.0 27.9 %step.1 = f32[2,5,256,128]{3,2,1,0:T(8,128)S(1)} custom-call(bf16[4,2,5,256,128]{4,3,2,1,0:T(8,128)(2,1)} %k_hbm.1, f32[2,5,256,128]{3,2,1,0:T(8,128)} %a_hbm.1, bf16[5,2,256,128]{3,2,1,0:T(8,128)(2,1)} %s_hbm.1, f32[2,2,256,128]{3,2,1,0:T(8,128)} %w_hbm.1, f32[4,4]{1,0:T(4,128)} %p_hbm.1, s32[1,4]{1,0:T(1,128)} %t_hbm.1), custom_call_target="tpu_custom_call" | custom-call | tf_op jit(solution)/shard_map/step/pallas_call | solution.py:471
  27.9 1.1 %copy.8 = f32[2,5,256,128]{3,2,1,0:T(8,128)} copy(f32[2,5,256,128]{3,2,1,0:T(8,128)S(1)} %step.1) | data formatting | bytes 2621440
